TPU v7x, 128 devices: a whole 4x4x4 slice. The times are simulated.
128 devices in a mesh: rows: 16 (over y_lo, x, core), band: 8 (over y_hi, z).
Axes of the slice: x: 4, y: 4 (y_hi: 2, y_lo: 2; y = y_hi * 2 + y_lo), z: 4, core: 2. Of those that a mesh axis runs over, the one named last changes fastest.
Arguments:
- pan_image: float32 [768, 12288], P('rows', 'band'), may hold values from -1 to 17
- vnir_bands: float32 [8, 192, 3072], P('band', 'rows'), may hold values from -13 to 13
- swir_bands: float32 [8, 64, 1024], P('band', 'rows'), may hold values from -12 to 12
Outputs:
- joined_vnir: float32 [8, 768, 12288], P(None, 'rows', 'band')
- joined_swir: float32 [8, 192, 3072], P(None, 'rows', 'band')
All inputs are finite; a program needn't handle non-finite values.
Results may differ from a plain program's by a relative error of at most 0.00023.
Values sent between devices are 32-bit elements; how exact they have to be, the bound alone decides.
A program may use at most 128 MiB of HBM per device.

v0:
```python
import functools
import math

import jax
import jax.numpy as jnp
import ml_dtypes
import numpy as np
from jax import lax
from jax.experimental import pallas as pl
from jax.experimental.pallas import tpu as pltpu
from jax.sharding import PartitionSpec as P

F32 = jnp.float32
BF16 = jnp.bfloat16
MESH = pl.DeviceIdType.MESH
VM = pltpu.VMEM

BANDS = 8
STRIPS = 16
BLOCKS = 8
HEIGHT = 768
WIDTH = 12288
N1 = float(HEIGHT * WIDTH)
N2 = float(HEIGHT * WIDTH // 16)
NYQUIST_GAIN = 0.29


def gauss_taps(upscale, kernel_len):
    spread = upscale * math.sqrt(-2.0 * math.log(NYQUIST_GAIN)) / math.pi
    radius = kernel_len // 2
    offsets = np.arange(-radius, radius + 1) * 1.0
    values = np.exp(-(offsets**2) / (2.0 * spread**2))
    return values / values.sum()


def cubic_weight(distance):
    distance = abs(distance)
    if distance <= 1.0:
        return 1.5 * distance**3 - 2.5 * distance**2 + 1.0
    if distance < 2.0:
        return -0.5 * distance**3 + 2.5 * distance**2 - 4.0 * distance + 2.0
    return 0.0


def cubic_table(upscale):
    weights = np.zeros((5, upscale))
    for phase_index in range(upscale):
        centre = (phase_index + 0.5) / upscale - 0.5
        first_tap = math.floor(centre)
        fraction = centre - first_tap
        for tap_index in range(-1, 3):
            weights[first_tap + tap_index + 2, phase_index] += cubic_weight(tap_index - fraction)
    return weights


C4 = cubic_table(4)
C3 = cubic_table(3)
G4 = gauss_taps(4, 17)
G3 = gauss_taps(3, 13)
MEAN_TAPS = C4.mean(axis=1)


def split(matrix):
    high = matrix.astype(np.float32).astype(ml_dtypes.bfloat16)
    low = (matrix - high.astype(np.float64)).astype(ml_dtypes.bfloat16)
    return high, low


def tables():
    up_rows = np.zeros((48, 16))
    for m in range(12):
        for p in range(4):
            for t in range(5):
                up_rows[4 * m + p, m + t] += C4[t, p]
    up_cols = np.zeros((1536, 512))
    for m in range(384):
        for p in range(4):
            for t in range(5):
                up_cols[4 * m + p, (m + t - 2) % 512] += C4[t, p]
    gram_rows = up_rows.T @ up_rows
    gram_cols = up_cols.T @ up_cols
    lanes = np.zeros((16, 512), np.float32)
    at = np.arange(512)
    for t in range(-4, 5):
        lanes[t + 4] = gram_cols[at, (at + t) % 512]
    lanes[9] = up_cols.sum(axis=0)
    row_sum = up_rows.sum(axis=0)

    low = np.zeros((96, 112))
    for f in range(96):
        for t in range(17):
            low[f, f + t] = G4[t]
    mean = np.zeros((24, 112))
    mean_low = np.zeros((24, 112))
    for i in range(24):
        mean[i, 8 + 4 * i : 12 + 4 * i] = 0.25
        mean_low[i] = low[4 * i : 4 * i + 4].mean(axis=0)
    g3_rows = np.zeros((12, 24))
    for i in range(12):
        g3_rows[i, i : i + 13] = G3
    row_stack = []
    for variant in range(3):
        keep = np.ones((24, 1))
        if variant == 0:
            keep[:6] = 0.0
        if variant == 2:
            keep[18:] = 0.0
        row_stack.append(
            np.concatenate(
                [
                    low[24:72],
                    up_rows.T @ low[24:72],
                    mean_low[6:18],
                    g3_rows @ (keep * mean_low),
                    mean[6:18],
                    g3_rows @ (keep * mean),
                ]
            )
        )
    rows_hi, rows_lo = split(np.stack(row_stack))

    low_cols = np.zeros((256, 128))
    for o in range(128):
        for t in range(-8, 9):
            q = o + t
            row = q if 0 <= q < 128 else (q if q >= 128 else 256 + q)
            low_cols[row, o] = G4[t + 8]
    mean_cols = np.zeros((640, 128))
    for f in range(512):
        mean_cols[f, f // 4] = 0.25
    for f in range(32):
        mean_cols[512 + f, f // 4] = 0.25
        mean_cols[512 + 96 + f, 120 + f // 4] = 0.25
    back_cols = np.zeros((640, 128))
    for n in range(128):
        for t in range(5):
            for p in range(4):
                f = 4 * (n - (t - 2)) + p
                row = f if f >= 0 else 640 + f
                back_cols[row, n] += C4[t, p]
    fine = np.zeros((256, 512))
    for m in range(128):
        for p in range(4):
            for t in range(5):
                fine[(m + t - 2) % 256, 4 * m + p] += C4[t, p]
    third = np.zeros((256, 384))
    for m in range(128):
        for p in range(3):
            for t in range(5):
                third[(m + t - 2) % 256, 3 * m + p] += C3[t, p]
    constants = (
        rows_hi,
        rows_lo,
        *split(low_cols),
        mean_cols.astype(ml_dtypes.bfloat16),
        *split(back_cols),
        *split(fine),
        *split(third),
        lanes,
    )
    return constants, gram_rows, row_sum, up_rows


CONSTANTS, GRAM_ROWS, ROW_SUM, UP_ROWS = tables()
NUM_CONST = len(CONSTANTS)


def halves(x):
    high = x.astype(BF16)
    return high, (x - high.astype(F32)).astype(BF16)


def mm(a, b):
    return jnp.dot(a, b, preferred_element_type=F32)


def dot3(x, high, low):
    xh, xl = halves(x)
    return mm(xh, high) + mm(xl, high) + mm(xh, low)


def dot2(x, exact):
    xh, xl = halves(x)
    return mm(xh, exact) + mm(xl, exact)


def lane(shape):
    return lax.broadcasted_iota(jnp.int32, shape, len(shape) - 1)


def edge(next_tile, prev_tile):
    return jnp.where(lane(next_tile.shape) < 64, next_tile, prev_tile)


def shifted(x, t):
    n = x.shape[1]
    return x if t == 0 else pltpu.roll(x, (-t) % n, 1)


def col_filter(x, taps):
    radius = len(taps) // 2
    total = float(taps[radius]) * x
    for t in range(-radius, radius + 1):
        if t:
            total = total + float(taps[t + radius]) * shifted(x, t)
    return total


def pick(e, strip, row, tile):
    return e[strip, tile, pl.ds(row, 8, stride=8), :]


def vnir_row(e, strip, i):
    if i < 8:
        parts = [pick(e, strip, i, t) for t in range(3)] + [pick(e, strip, i, 5)]
    else:
        j = i - 8
        parts = [
            pick(e, strip, j, 3),
            pick(e, strip, 4 + j, 3),
            pick(e, strip, j, 4),
            pltpu.roll(pick(e, strip, j, 5), 64, 1),
        ]
    return jnp.concatenate(parts, axis=1)


def swir_row(e, strip, j):
    return jnp.concatenate(
        [pick(e, strip, 4 + j, 4), pltpu.roll(pick(e, strip, 4 + j, 5), 64, 1)], axis=1
    )


def fold(x):
    total = x[:, 0:128]
    for t in range(1, x.shape[1] // 128):
        total = total + x[:, 128 * t : 128 * t + 128]
    return total


def pack(vs, ss, sb):
    for d in range(BLOCKS):
        left, right = 384 * d - 128, 384 * d + 384

        def halo(ref, rows, at, after, width):
            shape = (rows[1] - rows[0], 128)
            prev = ref[rows[0] : rows[1], at : at + 128] if at >= 0 else jnp.zeros(shape, F32)
            nxt = ref[rows[0] : rows[1], after : after + 128] if after < width else jnp.zeros(shape, F32)
            return edge(nxt, prev)

        for t in range(3):
            sb[d, t] = vs[0:8, 384 * d + 128 * t : 384 * d + 128 * t + 128]
        sb[d, 3, 0:4] = vs[8:12, 384 * d : 384 * d + 128]
        sb[d, 3, 4:8] = vs[8:12, 384 * d + 128 : 384 * d + 256]
        sb[d, 4, 0:4] = vs[8:12, 384 * d + 256 : 384 * d + 384]
        sb[d, 4, 4:8] = ss[0:4, 128 * d : 128 * d + 128]
        sb[d, 5, 0:4] = halo(vs, (8, 12), left, right, 3072)
        sb[d, 5, 4:8] = halo(ss, (0, 4), 128 * d - 128, 128 * d + 128, 1024)
        other = pltpu.roll(sb[d, 5], 64, 1)
        own = halo(vs, (0, 8), left, right, 3072)
        at = lane((8, 128))
        sb[d, 5] = jnp.where((at >= 32) & (at < 96), other, own)


def pan_stage(pan_ext, consts, variant, d_out, ts, dd):
    rows_hi, rows_lo, low_hi, low_lo, mean_c, back_hi, back_lo = consts[:7]
    halo = edge(pan_ext[:, 1664:1792], pan_ext[:, 1536:1664])
    full = jnp.concatenate([pan_ext[:, 0:1536], halo], axis=1)
    fh, fl = halves(full)
    rh, rl = rows_hi[variant], rows_lo[variant]
    q = mm(rh, fh) + mm(rh, fl) + mm(rl, fh)
    top = q[0:88]
    tiles = [top[:, 128 * j : 128 * j + 128] for j in range(13)]
    lhs = jnp.concatenate(
        [
            jnp.concatenate([tiles[j], edge(tiles[(j + 1) % 13], tiles[(j + 12) % 13])], axis=1)
            for j in range(13)
        ],
        axis=0,
    )
    low = dot3(lhs, low_hi[...], low_lo[...])
    low_tile = [low[88 * j : 88 * j + 88] for j in range(13)]
    total = jnp.zeros((8, 128), F32)
    for j in range(12):
        d_out[:, 128 * j : 128 * j + 128] = (
            pan_ext[32:80, 128 * j : 128 * j + 128] - low_tile[j][0:48]
        )
        for k in range(6):
            total = total + low_tile[j][8 * k : 8 * k + 8]
    zero = jnp.zeros((16, 128), F32)
    back = [low_tile[j][48:64] for j in range(12)] + [zero]
    lhs = jnp.concatenate(
        [
            jnp.concatenate(
                back[4 * t : 4 * t + 4] + [edge(back[4 * t + 4], back[(4 * t + 12) % 13])], axis=1
            )
            for t in range(3)
        ],
        axis=0,
    )
    main = dot3(lhs, back_hi[...], back_lo[...])
    rim = dot3(edge(back[0], back[11]), back_hi[512:640], back_lo[512:640])
    for t in range(3):
        ts[:, 128 * t : 128 * t + 128] = main[16 * t : 16 * t + 16]
    ts[:, 384:512] = rim
    diff = [q[88:112, 128 * j : 128 * j + 128] - low_tile[j][64:88] for j in range(13)]
    lhs = jnp.concatenate(
        [jnp.concatenate(diff[4 * t : 4 * t + 4], axis=1) for t in range(3)], axis=0
    )
    main = dot2(lhs, mean_c[0:512])
    for t in range(3):
        dd[0:24, 128 * t : 128 * t + 128] = main[24 * t : 24 * t + 24]
    dd[0:24, 384:512] = dot2(diff[12], mean_c[512:640])
    return total


def column_mask(block):
    at = lane((1, 512))
    left = jnp.where(block == 0, 0.0, 1.0)
    right = jnp.where(block == BLOCKS - 1, 0.0, 1.0)
    return jnp.where(at >= 448, left, jnp.where(at >= 384, right, 1.0))


def front_compute(e, pan_ext, consts, r, c, d_out, ts, dd, xs, ys, lvs, vl, swu, dl, rl):
    third_hi, third_lo, lanes = consts[9:12]
    variant = jnp.where(r == 0, 0, jnp.where(r == STRIPS - 1, 2, 1))
    sums = {}
    sums[10] = pan_stage(pan_ext, consts, variant, d_out, ts, dd)
    for k in range(28):
        strip, i = (0, k + 4) if k < 8 else ((1, k - 8) if k < 20 else (2, k - 20))
        xs[k] = vnir_row(e, strip, i)
    for i in range(16):
        total = None
        for j in range(16):
            if GRAM_ROWS[i, j] != 0.0:
                term = float(GRAM_ROWS[i, j]) * xs[j + 6]
                total = term if total is None else total + term
        y = lanes[4:5, :] * total
        for t in range(-4, 5):
            if t:
                y = y + lanes[t + 4 : t + 5, :] * shifted(total, t)
        ys[i] = y
    acc = [jnp.zeros((8, 128), F32) for _ in range(10)]
    ones = lanes[9:10, :]
    for i in range(16):
        x = xs[i + 6]
        for j in range(8):
            acc[j] = acc[j] + fold(x * ys[i, j : j + 1, :])
        acc[8] = acc[8] + fold(x * ts[i : i + 1, :])
        acc[9] = acc[9] + float(ROW_SUM[i]) * fold(x * ones)
    for k in range(10):
        sums[k] = acc[k]
    up_keep = jnp.where(r == 0, 0.0, 1.0)
    down_keep = jnp.where(r == STRIPS - 1, 0.0, 1.0)
    mask = column_mask(c)
    mean_rows = []
    for i in range(24):
        total = None
        for t in range(5):
            term = float(MEAN_TAPS[t]) * xs[i + t]
            total = term if total is None else total + term
        if i < 6:
            total = total * up_keep
        if i >= 18:
            total = total * down_keep
        mean_rows.append(total)
    for i in range(12):
        total = float(G3[6]) * mean_rows[i + 6]
        for t in range(6):
            total = total + float(G3[t]) * (mean_rows[i + t] + mean_rows[i + 12 - t])
        lowered = col_filter(total, MEAN_TAPS) * mask
        lowered = col_filter(lowered, G3)[:, 0:384]
        lvs[i] = lowered
        vl[i] = col_filter(mean_rows[i + 6], MEAN_TAPS)[:, 0:384] - lowered
    dcol = dd[8:24, :] * mask
    dcol = col_filter(dcol, G3)[:, 0:384]
    low_d = dcol[4:16]
    dl[...] = dd[0:12, 0:384] - low_d
    ts[0:12, 0:384] = low_d
    srow = [
        swir_row(e, *at)
        for at in ((0, 2), (0, 3), (1, 0), (1, 1), (1, 2), (1, 3), (2, 0), (2, 1))
    ]
    up = []
    for m in range(4):
        for p in range(3):
            total = None
            for t in range(5):
                if C3[t, p] != 0.0:
                    term = float(C3[t, p]) * srow[m + t]
                    total = term if total is None else total + term
            up.append(total)
    swu[...] = dot3(jnp.concatenate(up, axis=0), third_hi[...], third_lo[...])
    acc = [jnp.zeros((8, 128), F32) for _ in range(22)]
    for i in range(12):
        lv = lvs[i]
        sw = swu[8 * i : 8 * i + 8, :]
        ld = ts[i : i + 1, 0:384]
        for j in range(8):
            other = lvs[i, j : j + 1, :]
            acc[j] = acc[j] + fold(lv * other)
            acc[8 + j] = acc[8 + j] + fold(sw * other)
        acc[16] = acc[16] + fold(lv * ld)
        acc[17] = acc[17] + fold(sw * ld)
        acc[18] = acc[18] + fold(lv)
        acc[19] = acc[19] + fold(sw)
        acc[20] = acc[20] + fold(ld)
        acc[21] = acc[21] + fold(ld * ld)
    for k in range(22):
        sums[16 + k] = acc[k]
    at = lane((8, 128))
    packed = jnp.zeros((8, 128), F32)
    for k, value in sums.items():
        packed = jnp.where(at == k, jnp.sum(value, axis=1, keepdims=True), packed)
    rl[...] = packed


def upsample(xs, consts, zs, up_out):
    fine_hi, fine_lo = consts[7:9]
    for m in range(12):
        for p in range(4):
            total = None
            for t in range(5):
                if C4[t, p] != 0.0:
                    term = float(C4[t, p]) * xs[m + t + 6]
                    total = term if total is None else total + term
            for tile in range(4):
                zs[tile, pl.ds(4 * m + p, 8, stride=48), :] = total[
                    :, 128 * tile : 128 * tile + 128
                ]

    @pl.loop(0, BANDS)
    def _(b):
        at = pl.ds(pl.multiple_of(b * 48, 48), 48)
        z = [zs[k, at, :] for k in range(4)]
        lhs = jnp.concatenate(
            [
                jnp.concatenate([z[k], edge(z[k + 1], z[(k + 3) % 4])], axis=1)
                for k in range(3)
            ],
            axis=0,
        )
        up = dot3(lhs, fine_hi[...], fine_lo[...])
        for k in range(3):
            up_out[at, 512 * k : 512 * k + 512] = up[48 * k : 48 * k + 48]


def front_kernel(pan, vnir, swir, *rest):
    hbm_consts = rest[:NUM_CONST]
    rt, up_out, d_out, vl, swu, dl = rest[NUM_CONST : NUM_CONST + 6]
    rest = rest[NUM_CONST + 6 :]
    consts = rest[:NUM_CONST]
    (vs, ss, sb, e, pe, xs, ys, ts, dd, lvs, zs, rl, g1, mid, g2) = rest[NUM_CONST : NUM_CONST + 15]
    (csem, lsem, ssem, rsem, fsem, hsem, psem, qsem, g1s, g1r, g2s, g2r) = rest[NUM_CONST + 15 :]
    r = lax.axis_index("rows")
    c = lax.axis_index("band")

    def remote(src, dst, send, recv, row, block):
        return pltpu.make_async_remote_copy(
            src_ref=src, dst_ref=dst, send_sem=send, recv_sem=recv,
            device_id=(row, block), device_id_type=MESH,
        )

    rl8 = lax.rem(r, 8)
    base = r - rl8
    q = base + c
    barrier = pltpu.get_barrier_semaphore()

    def greet(row, block):
        pl.semaphore_signal(barrier, inc=1, device_id=(row, block), device_id_type=MESH)

    first = [(base + lax.rem(rl8 + k, 8), c) for k in range(1, 8)]
    second = []
    for k in range(1, 16):
        q2 = lax.rem(q + k, 16)
        c2 = lax.rem(q2, 8)
        second.append((q2 - c2 + rl8, c2))
    around = [(lax.rem(r + 1, STRIPS), c), (lax.rem(r + STRIPS - 1, STRIPS), c)]
    partners = first + second + around
    for row, block in partners:
        greet(row, block)

    loads = [
        pltpu.make_async_copy(vnir.at[0], vs, lsem.at[0]),
        pltpu.make_async_copy(swir.at[0], ss, lsem.at[1]),
        pltpu.make_async_copy(pan, pe.at[pl.ds(32, 48), pl.ds(0, 1536)], lsem.at[2]),
    ]
    for copy in loads:
        copy.start()
    const_loads = [
        pltpu.make_async_copy(hbm_consts[k], consts[k], csem.at[k]) for k in range(NUM_CONST)
    ]
    for copy in const_loads:
        copy.start()

    @pl.when(r == 0)
    def _():
        pe[0:32, :] = jnp.zeros((32, 1792), F32)
        e[0] = jnp.zeros((6, 64, 128), F32)

    @pl.when(r == STRIPS - 1)
    def _():
        pe[80:112, :] = jnp.zeros((32, 1792), F32)
        e[2] = jnp.zeros((6, 64, 128), F32)

    @pl.when(c == 0)
    def _():
        pe[32:80, 1536:1664] = jnp.zeros((48, 128), F32)

    @pl.when(c == BLOCKS - 1)
    def _():
        pe[32:80, 1664:1792] = jnp.zeros((48, 128), F32)

    loads[0].wait()
    loads[1].wait()
    pack(vs, ss, sb)
    loads[2].wait()
    pl.semaphore_wait(barrier, len(partners))

    def pan_cols(side):
        src = pe.at[pl.ds(32, 48), pl.ds(1408, 128)] if side == 0 else pan_first
        dst = pe.at[pl.ds(32, 48), pl.ds(1536 + 128 * side, 128)]
        block = c + 1 if side == 0 else c - 1
        return remote(src, dst, psem.at[side], qsem.at[side], r, block)

    pan_first = pe.at[pl.ds(32, 48), pl.ds(0, 128)]

    def pan_rows(side):
        src = pe.at[pl.ds(48, 32), pl.ds(0, 1536)] if side == 0 else pe.at[pl.ds(32, 32), pl.ds(0, 1536)]
        dst = pe.at[pl.ds(0, 32), pl.ds(0, 1536)] if side == 0 else pe.at[pl.ds(80, 32), pl.ds(0, 1536)]
        row = r + 1 if side == 0 else r - 1
        return remote(src, dst, psem.at[2 + side], qsem.at[2 + side], row, c)

    def pan_corner(side):
        src = pe.at[pl.ds(48, 32), pl.ds(1536, 256)] if side == 0 else pe.at[pl.ds(32, 32), pl.ds(1536, 256)]
        dst = pe.at[pl.ds(0, 32), pl.ds(1536, 256)] if side == 0 else pe.at[pl.ds(80, 32), pl.ds(1536, 256)]
        row = r + 1 if side == 0 else r - 1
        return remote(src, dst, psem.at[4 + side], qsem.at[4 + side], row, c)

    has_below, has_above = r < STRIPS - 1, r > 0
    has_right, has_left = c < BLOCKS - 1, c > 0

    def when(cond, action):
        @pl.when(cond)
        def _():
            action()

    when(has_right, lambda: pan_cols(0).start())
    when(has_left, lambda: pan_cols(1).start())

    def band_rows(b):
        return pl.ds(pl.multiple_of(b * 8, 8), 8)

    def block_send(k):
        block = lax.rem(c + k, 8)
        return remote(sb.at[block], e.at[1, pl.ds(0, 6), band_rows(c)], ssem.at[k], rsem.at[k], r, block)

    def block_recv(k):
        b = lax.rem(c + 8 - k, 8)
        return remote(sb.at[0], e.at[1, pl.ds(0, 6), band_rows(b)], ssem.at[k], rsem.at[k], r, c)

    def forward(k, side):
        b = lax.rem(c + 8 - k, 8)
        dst = e.at[2 * side, pl.ds(0, 6), band_rows(b)]
        src = sb.at[c] if k == 0 else e.at[1, pl.ds(0, 6), band_rows(b)]
        row = r + 1 if side == 0 else r - 1
        return remote(src, dst, fsem.at[side, k], hsem.at[side, k], row, c)

    order = (4, 3, 5, 2, 6, 1, 7)
    for k in order:
        block_send(k).start()
    own = pltpu.make_async_copy(sb.at[c], e.at[1, pl.ds(0, 6), band_rows(c)], lsem.at[3])
    own.start()
    when(has_below, lambda: forward(0, 0).start())
    when(has_above, lambda: forward(0, 1).start())
    when(has_below, lambda: pan_rows(0).start())
    when(has_above, lambda: pan_rows(1).start())

    when(has_left, lambda: pan_cols(0).wait_recv())
    when(has_right, lambda: pan_cols(1).wait_recv())
    when(has_below, lambda: pan_corner(0).start())
    when(has_above, lambda: pan_corner(1).start())
    for k in (1, 7, 2, 6, 3, 5, 4):
        block_recv(k).wait_recv()
        when(has_below, functools.partial(lambda k: forward(k, 0).start(), k))
        when(has_above, functools.partial(lambda k: forward(k, 1).start(), k))
    own.wait()
    for copy in const_loads:
        copy.wait()
    when(has_above, lambda: (pan_rows(0).wait_recv(), pan_corner(0).wait_recv()))
    when(has_below, lambda: (pan_rows(1).wait_recv(), pan_corner(1).wait_recv()))
    for k in range(8):
        when(has_above, functools.partial(lambda k: forward(k, 0).wait_recv(), k))
        when(has_below, functools.partial(lambda k: forward(k, 1).wait_recv(), k))

    front_compute(e, pe, consts, r, c, d_out, ts, dd, xs, ys, lvs, vl, swu, dl, rl)

    def sum_one(k):
        row, block = first[k - 1]
        return remote(rl, g1.at[rl8], g1s.at[k], g1r.at[k], row, block)

    def sum_one_recv(k):
        return remote(rl, g1.at[lax.rem(rl8 + 8 - k, 8)], g1s.at[k], g1r.at[k], r, c)

    def sum_two(k):
        row, block = second[k - 1]
        return remote(mid, g2.at[q_slot], g2s.at[k], g2r.at[k], row, block)

    def sum_two_recv(k):
        return remote(mid, g2.at[lax.rem(q_slot + 16 - k, 16)], g2s.at[k], g2r.at[k], r, c)

    q_slot = q
    for k in range(1, 8):
        sum_one(k).start()
    g1[rl8] = rl[...]
    for k in range(1, 8):
        sum_one_recv(k).wait_recv()
    total = g1[0]
    for k in range(1, 8):
        total = total + g1[k]
    mid[...] = total
    for k in range(1, 16):
        sum_two(k).start()
    g2[q_slot] = total
    upsample(xs, consts, zs, up_out)
    for k in range(1, 16):
        sum_two_recv(k).wait_recv()
    total = g2[0]
    for k in range(1, 16):
        total = total + g2[k]
    rt[...] = total

    for k in range(1, 8):
        block_send(k).wait_send()
        sum_one(k).wait_send()
    for k in range(1, 16):
        sum_two(k).wait_send()
    when(has_right, lambda: pan_cols(0).wait_send())
    when(has_left, lambda: pan_cols(1).wait_send())
    for side, cond in ((0, has_below), (1, has_above)):
        when(cond, functools.partial(lambda side: (pan_rows(side).wait_send(), pan_corner(side).wait_send()), side))
        for k in range(8):
            when(cond, functools.partial(lambda k, side: forward(k, side).wait_send(), k, side))


def front(pan, vnir, swir):
    return pl.pallas_call(
        front_kernel,
        name="front",
        out_shape=[
            jax.ShapeDtypeStruct((8, 128), F32),
            jax.ShapeDtypeStruct((384, 1536), F32),
            jax.ShapeDtypeStruct((48, 1536), F32),
            jax.ShapeDtypeStruct((12, 8, 384), F32),
            jax.ShapeDtypeStruct((96, 384), F32),
            jax.ShapeDtypeStruct((12, 384), F32),
        ],
        in_specs=[pl.BlockSpec(memory_space=pl.ANY)] * (3 + NUM_CONST),
        out_specs=[pl.BlockSpec(memory_space=VM)] * 6,
        scratch_shapes=[VM(k.shape, BF16 if k.dtype == ml_dtypes.bfloat16 else F32) for k in CONSTANTS]
        + [
            VM((12, 3072), F32),
            VM((4, 1024), F32),
            VM((8, 6, 8, 128), F32),
            VM((3, 6, 64, 128), F32),
            VM((112, 1792), F32),
            VM((28, 8, 512), F32),
            VM((16, 8, 512), F32),
            VM((16, 512), F32),
            VM((24, 512), F32),
            VM((12, 8, 384), F32),
            VM((4, 384, 128), F32),
            VM((8, 128), F32),
            VM((8, 8, 128), F32),
            VM((8, 128), F32),
            VM((16, 8, 128), F32),
            pltpu.SemaphoreType.DMA((NUM_CONST,)),
            pltpu.SemaphoreType.DMA((4,)),
            pltpu.SemaphoreType.DMA((8,)),
            pltpu.SemaphoreType.DMA((8,)),
            pltpu.SemaphoreType.DMA((2, 8)),
            pltpu.SemaphoreType.DMA((2, 8)),
            pltpu.SemaphoreType.DMA((6,)),
            pltpu.SemaphoreType.DMA((6,)),
            pltpu.SemaphoreType.DMA((8,)),
            pltpu.SemaphoreType.DMA((8,)),
            pltpu.SemaphoreType.DMA((16,)),
            pltpu.SemaphoreType.DMA((16,)),
        ],
        compiler_params=pltpu.CompilerParams(
            collective_id=0, has_side_effects=True, vmem_limit_bytes=56 << 20
        ),
    )(pan, vnir, swir, *[jnp.asarray(k) for k in CONSTANTS])


def solve_spd(a, b):
    a = [list(row) for row in a]
    inverse = []
    factor = [[None] * 8 for _ in range(8)]
    for j in range(8):
        inv = 1.0 / a[j][j]
        inverse.append(inv)
        for i in range(j + 1, 8):
            factor[i][j] = a[i][j] * inv
        for i in range(j + 1, 8):
            for k in range(j + 1, i + 1):
                a[i][k] = a[i][k] - factor[i][j] * a[k][j]
    z = list(b)
    for j in range(8):
        for i in range(j + 1, 8):
            z[i] = z[i] - factor[i][j] * z[j]
    z = [z[j] * inverse[j] for j in range(8)]
    for j in range(7, -1, -1):
        for i in range(j):
            z[i] = z[i] - factor[j][i] * z[j]
    return z


def total_of(values):
    total = values[0]
    for value in values[1:]:
        total = total + value
    return total


def solve(rt, cb):
    for k in range(38):
        if k < 11 or k >= 16:
            cb[k] = jnp.broadcast_to(rt[:, k : k + 1], (8, 128))

    def at(k, i):
        return cb[k, i : i + 1, :]

    mean = [at(9, i) * (1.0 / N1) for i in range(8)]
    mean_p = jnp.sum(cb[10], axis=0, keepdims=True) * (1.0 / N1)
    a = [[at(j, i) * (1.0 / N1) - mean[i] * mean[j] for j in range(i + 1)] for i in range(8)]
    b = [at(8, i) * (1.0 / N1) - mean[i] * mean_p for i in range(8)]
    w = solve_spd(a, b)
    scale = 1.0 / total_of([b[i] * w[i] for i in range(8)])
    gain = [b[i] * scale for i in range(8)]
    sum_d = at(36, 0)
    sum_dd = at(37, 0)
    q = [at(32, i) for i in range(8)]
    mean2 = [(at(34, i) + gain[i] * sum_d) * (1.0 / N2) for i in range(8)]
    a2 = [
        [
            (at(16 + j, i) + gain[i] * q[j] + gain[j] * q[i] + gain[i] * gain[j] * sum_dd) * (1.0 / N2)
            - mean2[i] * mean2[j]
            for j in range(i + 1)
        ]
        for i in range(8)
    ]
    swir_mean = cb[35] * (1.0 / N2)
    cross = [
        (cb[24 + i] + gain[i] * cb[33]) * (1.0 / N2) - mean2[i] * swir_mean for i in range(8)
    ]
    y = [jnp.sum(cross[i], axis=0, keepdims=True) * 0.125 for i in range(8)]
    v = solve_spd(a2, y)
    share = total_of([v[i] * cross[i] for i in range(8)]) / total_of([v[i] * y[i] for i in range(8)])
    return gain, v, share


def wide(x, copies):
    return jnp.concatenate([x] * copies, axis=1)


def back_kernel(rt, up, d, vl, swu, dl, joined, joined_swir, cb, gs, out, swir_out, sem):
    gain, v, share = solve(rt, cb)
    for b in range(8):
        gs[b] = jnp.broadcast_to(gain[b], (8, 128))

    @pl.loop(0, BANDS)
    def _(b):
        g = wide(gs[b], 2)
        rows = pl.multiple_of(b * 48, 48)
        for i in range(6):
            for t in range(6):
                at = slice(256 * t, 256 * t + 256)
                out[b, 8 * i : 8 * i + 8, at] = (
                    up[pl.ds(rows + 8 * i, 8), at] + g * d[8 * i : 8 * i + 8, at]
                )
        pltpu.make_async_copy(out.at[b], joined.at[b], sem.at[b]).start()

    row8 = lax.broadcasted_iota(jnp.int32, (8, 128), 0)
    v8 = jnp.zeros((8, 128), F32)
    for b in range(8):
        v8 = jnp.where(row8 == b, jnp.broadcast_to(v[b], (8, 128)), v8)
    v8 = wide(v8, 3)
    vg = wide(total_of([v[b] * gain[b] for b in range(8)]), 3)
    share3 = wide(share, 3)
    for i in range(12):
        detail = jnp.sum(v8 * vl[i], axis=0, keepdims=True) + vg * dl[i : i + 1, :]
        row = swu[8 * i : 8 * i + 8, :] + share3 * detail
        for t in range(3):
            swir_out[t, pl.ds(i, 8, stride=16), :] = row[:, 128 * t : 128 * t + 128]
    for s in range(8):
        for t in range(3):
            joined_swir[s, :, 128 * t : 128 * t + 128] = swir_out[t, 16 * s : 16 * s + 12, :]

    @pl.loop(0, BANDS)
    def _(b):
        pltpu.make_async_copy(out.at[b], joined.at[b], sem.at[b]).wait()


def back(rt, up, d, vl, swu, dl):
    return pl.pallas_call(
        back_kernel,
        name="back",
        out_shape=[
            jax.ShapeDtypeStruct((8, 48, 1536), F32),
            jax.ShapeDtypeStruct((8, 12, 384), F32),
        ],
        in_specs=[pl.BlockSpec(memory_space=VM)] * 6,
        out_specs=[pl.BlockSpec(memory_space=pl.ANY), pl.BlockSpec(memory_space=VM)],
        scratch_shapes=[
            VM((38, 8, 128), F32),
            VM((8, 8, 128), F32),
            VM((8, 48, 1536), F32),
            VM((3, 128, 128), F32),
            pltpu.SemaphoreType.DMA((8,)),
        ],
        compiler_params=pltpu.CompilerParams(vmem_limit_bytes=32 << 20),
    )(rt, up, d, vl, swu, dl)


def local(pan, vnir, swir):
    return tuple(back(*front(pan, vnir, swir)))


def solution(mesh):
    return jax.shard_map(
        local,
        mesh=mesh,
        in_specs=(P("rows", "band"), P("band", "rows", None), P("band", "rows", None)),
        out_specs=(P(None, "rows", "band"), P(None, "rows", "band")),
        check_vma=False,
    )
```

profile of v0, /device:TPU:1, one launch (start us, length us, event | category | flops | bytes accessed | tf_op | source)
XLA Modules:
  0.0 44.3 jit_solution(9660213070284619107)
XLA Ops:
  0.6 1.6 %copy.17.vnir = f32[1,12,3072]{2,1,0:T(8,128)} copy(f32[1,12,3072]{2,0,1:T(1,128)} %param.16) | data formatting | bytes 294912 | tf_op args[1]
  2.2 33.6 %front.1 = (f32[8,128]{1,0:T(8,128)}, f32[384,1536]{1,0:T(8,128)}, f32[48,1536]{1,0:T(8,128)}, f32[12,8,384]{2,1,0:T(8,128)}, f32[96,384]{1,0:T(8,128)}, /*index=5*/f32[12,384]{1,0:T(8,128)}) custom-call(f32[48,1536]{1,0:T(8,128)} %pan.1, f32[1,12,3072]{2,1,0:T(8,128)} %copy.17.vnir, f32[1,4,1024]{2,1,0:T(4,128)} %swir.1, ...), custom_call_target="tpu_custom_call" | custom-call | tf_op jit(solution)/shard_map/front/pallas_call | solution.py:646
  35.9 0.0 copy-start
  35.9 1.7 %copy-done = f32[384,1536]{1,0:T(8,128)S(1)} copy-done((f32[384,1536]{1,0:T(8,128)S(1)}, f32[384,1536]{1,0:T(8,128)}, u32[]{:S(2)}) %copy-start) | copy-done | bytes 2359320
  37.6 0.0 copy-start.1
  37.6 1.0 %copy-done.1 = f32[48,1536]{1,0:T(8,128)S(1)} copy-done((f32[48,1536]{1,0:T(8,128)S(1)}, f32[48,1536]{1,0:T(8,128)}, u32[]{:S(2)}) %copy-start.1) | copy-done | bytes 294936
  38.5 0.0 copy-start.2
  38.5 0.9 %copy-done.2 = f32[12,8,384]{2,1,0:T(8,128)S(1)} copy-done((f32[12,8,384]{2,1,0:T(8,128)S(1)}, f32[12,8,384]{2,1,0:T(8,128)}, u32[]{:S(2)}) %copy-start.2) | copy-done | bytes 147480
  39.4 0.0 copy-start.3
  39.4 0.9 %copy-done.3 = f32[96,384]{1,0:T(8,128)S(1)} copy-done((f32[96,384]{1,0:T(8,128)S(1)}, f32[96,384]{1,0:T(8,128)}, u32[]{:S(2)}) %copy-start.3) | copy-done | bytes 147480
  40.3 0.0 copy-start.4
  40.3 0.7 %copy-done.4 = f32[12,384]{1,0:T(8,128)S(1)} copy-done((f32[12,384]{1,0:T(8,128)S(1)}, f32[12,384]{1,0:T(8,128)}, u32[]{:S(2)}) %copy-start.4) | copy-done | bytes 18456
  41.1 0.0 copy-start.5
  41.1 0.7 %copy-done.5 = f32[8,128]{1,0:T(8,128)S(1)} copy-done((f32[8,128]{1,0:T(8,128)S(1)}, f32[8,128]{1,0:T(8,128)}, u32[]{:S(2)}) %copy-start.5) | copy-done | bytes 4120
  41.8 1.8 %back.1 = (f32[8,48,1536]{2,1,0:T(8,128)}, f32[8,12,384]{2,1,0:T(8,128)S(1)}) custom-call(f32[8,128]{1,0:T(8,128)S(1)} %copy-done.5, f32[384,1536]{1,0:T(8,128)S(1)} %copy-done, f32[48,1536]{1,0:T(8,128)S(1)} %copy-done.1, f32[12,8,384]{2,1,0:T(8,128)S(1)} %copy-done.2, f32[96,384]{1,0:T(8,128)S(1)} %copy-done.3, f32[12,384]{1,0:T(8,128)S(1)} %copy-done.4), custom_call_target="tpu_custom_call" | custom-call | tf_op jit(solution)/shard_map/back/pallas_call | solution.py:805
  43.6 0.7 %copy.18 = f32[8,12,384]{2,0,1:T(8,128)} copy(f32[8,12,384]{2,1,0:T(8,128)S(1)} %get-tuple-element.15) | data formatting | bytes 294912 | tf_op jit(solution)/shard_map/back/pallas_call | solution.py:805
Async XLA Ops:
  35.9 1.7 %copy-start = (f32[384,1536]{1,0:T(8,128)S(1)}, f32[384,1536]{1,0:T(8,128)}, u32[]{:S(2)}) copy-start(f32[384,1536]{1,0:T(8,128)} %get-tuple-element.9.up) | copy-start | bytes 7077892
  37.6 1.0 %copy-start.1 = (f32[48,1536]{1,0:T(8,128)S(1)}, f32[48,1536]{1,0:T(8,128)}, u32[]{:S(2)}) copy-start(f32[48,1536]{1,0:T(8,128)} %get-tuple-element.10.d) | copy-start | bytes 884740
  38.5 0.9 %copy-start.2 = (f32[12,8,384]{2,1,0:T(8,128)S(1)}, f32[12,8,384]{2,1,0:T(8,128)}, u32[]{:S(2)}) copy-start(f32[12,8,384]{2,1,0:T(8,128)} %get-tuple-element.11.vl) | copy-start | bytes 442372
  39.4 0.9 %copy-start.3 = (f32[96,384]{1,0:T(8,128)S(1)}, f32[96,384]{1,0:T(8,128)}, u32[]{:S(2)}) copy-start(f32[96,384]{1,0:T(8,128)} %get-tuple-element.12.swu) | copy-start | bytes 442372
  40.3 0.7 %copy-start.4 = (f32[12,384]{1,0:T(8,128)S(1)}, f32[12,384]{1,0:T(8,128)}, u32[]{:S(2)}) copy-start(f32[12,384]{1,0:T(8,128)} %get-tuple-element.13.dl) | copy-start | bytes 55300
  41.1 0.7 %copy-start.5 = (f32[8,128]{1,0:T(8,128)S(1)}, f32[8,128]{1,0:T(8,128)}, u32[]{:S(2)}) copy-start(f32[8,128]{1,0:T(8,128)} %get-tuple-element.8.rt) | copy-start | bytes 12292
where the time goes:
time: 44.7 us; the launch traced here: 44.3 us
  Pallas kernels  35.5 us (79%)
  local copies, waits for them, and re-layouts  8.18 us (18%)
  between operations  0.66 us (1%)
    pallas_call x1, Pallas kernels, front(): pl.pallas_call(front_kernel, name='front', out_shape=[jax.ShapeDtypeStruc...  33.6 us
    unnamed x13, local copies, waits for them, and re-layouts  7.47 us
    pallas_call x1, Pallas kernels, back(): pl.pallas_call(back_kernel, name='back', out_shape=[jax.ShapeDtypeStruct(...  1.83 us

commit v1 on v0

--- a/solution.py
+++ b/solution.py
@@ -238,26 +238,26 @@
 
 
 def pack(vs, ss, sb):
+    at = lane((8, 128))
+    zero = jnp.zeros((8, 128), F32)
+
+    def coarse(first, tile):
+        return vs[pl.ds(24 * first + tile, 8, stride=24), :] if 0 <= tile < 24 else zero
+
+    def short(tile):
+        return ss[0:4, 128 * tile : 128 * tile + 128] if 0 <= tile < 8 else zero[0:4]
+
     for d in range(BLOCKS):
-        left, right = 384 * d - 128, 384 * d + 384
-
-        def halo(ref, rows, at, after, width):
-            shape = (rows[1] - rows[0], 128)
-            prev = ref[rows[0] : rows[1], at : at + 128] if at >= 0 else jnp.zeros(shape, F32)
-            nxt = ref[rows[0] : rows[1], after : after + 128] if after < width else jnp.zeros(shape, F32)
-            return edge(nxt, prev)
-
         for t in range(3):
-            sb[d, t] = vs[0:8, 384 * d + 128 * t : 384 * d + 128 * t + 128]
-        sb[d, 3, 0:4] = vs[8:12, 384 * d : 384 * d + 128]
-        sb[d, 3, 4:8] = vs[8:12, 384 * d + 128 : 384 * d + 256]
-        sb[d, 4, 0:4] = vs[8:12, 384 * d + 256 : 384 * d + 384]
-        sb[d, 4, 4:8] = ss[0:4, 128 * d : 128 * d + 128]
-        sb[d, 5, 0:4] = halo(vs, (8, 12), left, right, 3072)
-        sb[d, 5, 4:8] = halo(ss, (0, 4), 128 * d - 128, 128 * d + 128, 1024)
+            sb[d, t] = coarse(0, 3 * d + t)
+        sb[d, 3, 0:4] = coarse(8, 3 * d)[0:4]
+        sb[d, 3, 4:8] = coarse(8, 3 * d + 1)[0:4]
+        sb[d, 4, 0:4] = coarse(8, 3 * d + 2)[0:4]
+        sb[d, 4, 4:8] = short(d)
+        sb[d, 5, 0:4] = edge(coarse(8, 3 * d + 3), coarse(8, 3 * d - 1))[0:4]
+        sb[d, 5, 4:8] = edge(short(d + 1), short(d - 1))
         other = pltpu.roll(sb[d, 5], 64, 1)
-        own = halo(vs, (0, 8), left, right, 3072)
-        at = lane((8, 128))
+        own = edge(coarse(0, 3 * d + 3), coarse(0, 3 * d - 1))
         sb[d, 5] = jnp.where((at >= 32) & (at < 96), other, own)
 
 
@@ -480,7 +480,7 @@
         greet(row, block)
 
     loads = [
-        pltpu.make_async_copy(vnir.at[0], vs, lsem.at[0]),
+        pltpu.make_async_copy(vnir, vs.at[pl.ds(0, 288)], lsem.at[0]),
         pltpu.make_async_copy(swir.at[0], ss, lsem.at[1]),
         pltpu.make_async_copy(pan, pe.at[pl.ds(32, 48), pl.ds(0, 1536)], lsem.at[2]),
     ]
@@ -647,18 +647,18 @@
         front_kernel,
         name="front",
         out_shape=[
-            jax.ShapeDtypeStruct((8, 128), F32),
-            jax.ShapeDtypeStruct((384, 1536), F32),
-            jax.ShapeDtypeStruct((48, 1536), F32),
-            jax.ShapeDtypeStruct((12, 8, 384), F32),
-            jax.ShapeDtypeStruct((96, 384), F32),
-            jax.ShapeDtypeStruct((12, 384), F32),
+            VM((8, 128), F32),
+            VM((384, 1536), F32),
+            VM((48, 1536), F32),
+            VM((12, 8, 384), F32),
+            VM((96, 384), F32),
+            VM((12, 384), F32),
         ],
         in_specs=[pl.BlockSpec(memory_space=pl.ANY)] * (3 + NUM_CONST),
         out_specs=[pl.BlockSpec(memory_space=VM)] * 6,
         scratch_shapes=[VM(k.shape, BF16 if k.dtype == ml_dtypes.bfloat16 else F32) for k in CONSTANTS]
         + [
-            VM((12, 3072), F32),
+            VM((384, 128), F32),
             VM((4, 1024), F32),
             VM((8, 6, 8, 128), F32),
             VM((3, 6, 64, 128), F32),
@@ -763,7 +763,7 @@
     return jnp.concatenate([x] * copies, axis=1)
 
 
-def back_kernel(rt, up, d, vl, swu, dl, joined, joined_swir, cb, gs, out, swir_out, sem):
+def back_kernel(rt, up, d, vl, swu, dl, joined, joined_swir, cb, gs, out, sem):
     gain, v, share = solve(rt, cb)
     for b in range(8):
         gs[b] = jnp.broadcast_to(gain[b], (8, 128))
@@ -789,12 +789,7 @@
     share3 = wide(share, 3)
     for i in range(12):
         detail = jnp.sum(v8 * vl[i], axis=0, keepdims=True) + vg * dl[i : i + 1, :]
-        row = swu[8 * i : 8 * i + 8, :] + share3 * detail
-        for t in range(3):
-            swir_out[t, pl.ds(i, 8, stride=16), :] = row[:, 128 * t : 128 * t + 128]
-    for s in range(8):
-        for t in range(3):
-            joined_swir[s, :, 128 * t : 128 * t + 128] = swir_out[t, 16 * s : 16 * s + 12, :]
+        joined_swir[i] = swu[8 * i : 8 * i + 8, :] + share3 * detail
 
     @pl.loop(0, BANDS)
     def _(b):
@@ -807,7 +802,7 @@
         name="back",
         out_shape=[
             jax.ShapeDtypeStruct((8, 48, 1536), F32),
-            jax.ShapeDtypeStruct((8, 12, 384), F32),
+            jax.ShapeDtypeStruct((12, 8, 384), F32),
         ],
         in_specs=[pl.BlockSpec(memory_space=VM)] * 6,
         out_specs=[pl.BlockSpec(memory_space=pl.ANY), pl.BlockSpec(memory_space=VM)],
@@ -815,7 +810,6 @@
             VM((38, 8, 128), F32),
             VM((8, 8, 128), F32),
             VM((8, 48, 1536), F32),
-            VM((3, 128, 128), F32),
             pltpu.SemaphoreType.DMA((8,)),
         ],
         compiler_params=pltpu.CompilerParams(vmem_limit_bytes=32 << 20),
@@ -823,7 +817,8 @@
 
 
 def local(pan, vnir, swir):
-    return tuple(back(*front(pan, vnir, swir)))
+    joined, rows = back(*front(pan, vnir.reshape(288, 128), swir))
+    return joined, jnp.swapaxes(rows, 0, 1)
 
 
 def solution(mesh):

time: 44.7 us -> 35.5 us (0.79)
  local copies, waits for them, and re-layouts: 8.18 us -> 0 us
  Pallas kernels: 35.5 us -> 34.7 us
    unnamed x13 -> x0, local copies, waits for them, and re-layouts: 7.47 us -> none
    pallas_call x1, Pallas kernels: 33.6 us -> 32.2 us  [front(): pl.pallas_call(front_kernel, name='front', out_shape=[VM((8, 128), F32),...]
    pallas_call x1 -> x0, local copies, waits for them, and re-layouts: 0.71 us -> none  [back(): pl.pallas_call(back_kernel, name='back', out_shape=[jax.ShapeDtypeStruct(...]
    pallas_call x1, Pallas kernels: 1.83 us -> 2.49 us  [back(): pl.pallas_call(back_kernel, name='back', out_shape=[jax.ShapeDtypeStruct(...]
where the time goes in v1:
time: 35.5 us; the launch traced here: 35.4 us
  Pallas kernels  34.7 us (98%)
  between operations  0.64 us (2%)
    pallas_call x1, Pallas kernels, front(): pl.pallas_call(front_kernel, name='front', out_shape=[VM((8, 128), F32),...  32.2 us
    pallas_call x1, Pallas kernels, back(): pl.pallas_call(back_kernel, name='back', out_shape=[jax.ShapeDtypeStruct(...  2.49 us

profile of v1, /device:TPU:1, one launch (start us, length us, event | category | flops | bytes accessed | tf_op | source)
XLA Modules:
  0.0 35.4 jit_solution(13184209969741171466)
XLA Ops:
  0.6 32.2 %front.1 = (f32[8,128]{1,0:T(8,128)S(1)}, f32[384,1536]{1,0:T(8,128)S(1)}, f32[48,1536]{1,0:T(8,128)S(1)}, f32[12,8,384]{2,1,0:T(8,128)S(1)}, f32[96,384]{1,0:T(8,128)S(1)}, /*index=5*/f32[12,384]{1,0:T(8,128)S(1)}) custom-call(f32[48,1536]{1,0:T(8,128)} %pan.1, f32[288,128]{1,0:T(8,128)} %bitcast.2, f32[1,4,1024]{2,1,0:T(4,128)} %swir.1, ...), custom_call_target="tpu_custom_call" | custom-call | tf_op jit(solution)/shard_map/front/pallas_call | solution.py:646
  32.9 2.5 %back.1 = (f32[8,48,1536]{2,1,0:T(8,128)}, f32[12,8,384]{2,1,0:T(8,128)}) custom-call(f32[8,128]{1,0:T(8,128)S(1)} %get-tuple-element.10.rt, f32[384,1536]{1,0:T(8,128)S(1)} %get-tuple-element.11.up, f32[48,1536]{1,0:T(8,128)S(1)} %get-tuple-element.12.d, f32[12,8,384]{2,1,0:T(8,128)S(1)} %get-tuple-element.13.vl, f32[96,384]{1,0:T(8,128)S(1)} %get-tuple-element.14.swu, ...), custom_call_target="tpu_custom_call" | custom-call | tf_op jit(solution)/shard_map/back/pallas_call | solution.py:800

commit v2 on v1

--- a/solution.py
+++ b/solution.py
@@ -320,25 +320,51 @@
     return jnp.where(at >= 448, left, jnp.where(at >= 384, right, 1.0))
 
 
-def front_compute(e, pan_ext, consts, r, c, d_out, ts, dd, xs, ys, lvs, vl, swu, dl, rl):
+def mean_row(xs, i):
+    total = None
+    for t in range(5):
+        term = float(MEAN_TAPS[t]) * xs[i + t]
+        total = term if total is None else total + term
+    return total
+
+
+def gram_cols(lanes, x):
+    y = lanes[4:5, :] * x
+    for t in range(-4, 5):
+        if t:
+            y = y + lanes[t + 4 : t + 5, :] * shifted(x, t)
+    return y
+
+
+def early_compute(e, pan_ext, consts, r, d_out, ts, dd, xs, xc, vl):
+    lanes = consts[11]
+    variant = jnp.where(r == 0, 0, jnp.where(r == STRIPS - 1, 2, 1))
+    for i in range(12):
+        row = vnir_row(e, 1, i)
+        xs[i + 8] = row
+        xc[i + 2] = gram_cols(lanes, row)
+    for i in range(2, 10):
+        vl[i] = col_filter(mean_row(xs, i + 6), MEAN_TAPS)[:, 0:384]
+    return pan_stage(pan_ext, consts, variant, d_out, ts, dd)
+
+
+def front_compute(e, consts, pan_sum, r, c, ts, dd, xs, xc, ys, lvs, vl, swu, dl, rl):
     third_hi, third_lo, lanes = consts[9:12]
-    variant = jnp.where(r == 0, 0, jnp.where(r == STRIPS - 1, 2, 1))
-    sums = {}
-    sums[10] = pan_stage(pan_ext, consts, variant, d_out, ts, dd)
+    sums = {10: pan_sum[...]}
     for k in range(28):
-        strip, i = (0, k + 4) if k < 8 else ((1, k - 8) if k < 20 else (2, k - 20))
-        xs[k] = vnir_row(e, strip, i)
+        if k < 8:
+            xs[k] = vnir_row(e, 0, k + 4)
+        elif k >= 20:
+            xs[k] = vnir_row(e, 2, k - 20)
+    for i in (0, 1, 14, 15):
+        xc[i] = gram_cols(lanes, xs[i + 6])
     for i in range(16):
         total = None
         for j in range(16):
             if GRAM_ROWS[i, j] != 0.0:
-                term = float(GRAM_ROWS[i, j]) * xs[j + 6]
+                term = float(GRAM_ROWS[i, j]) * xc[j]
                 total = term if total is None else total + term
-        y = lanes[4:5, :] * total
-        for t in range(-4, 5):
-            if t:
-                y = y + lanes[t + 4 : t + 5, :] * shifted(total, t)
-        ys[i] = y
+        ys[i] = total
     acc = [jnp.zeros((8, 128), F32) for _ in range(10)]
     ones = lanes[9:10, :]
     for i in range(16):
@@ -354,10 +380,7 @@
     mask = column_mask(c)
     mean_rows = []
     for i in range(24):
-        total = None
-        for t in range(5):
-            term = float(MEAN_TAPS[t]) * xs[i + t]
-            total = term if total is None else total + term
+        total = mean_row(xs, i)
         if i < 6:
             total = total * up_keep
         if i >= 18:
@@ -370,7 +393,10 @@
         lowered = col_filter(total, MEAN_TAPS) * mask
         lowered = col_filter(lowered, G3)[:, 0:384]
         lvs[i] = lowered
-        vl[i] = col_filter(mean_rows[i + 6], MEAN_TAPS)[:, 0:384] - lowered
+        if 2 <= i < 10:
+            vl[i] = vl[i] - lowered
+        else:
+            vl[i] = col_filter(mean_rows[i + 6], MEAN_TAPS)[:, 0:384] - lowered
     dcol = dd[8:24, :] * mask
     dcol = col_filter(dcol, G3)[:, 0:384]
     low_d = dcol[4:16]
@@ -449,8 +475,10 @@
     rt, up_out, d_out, vl, swu, dl = rest[NUM_CONST : NUM_CONST + 6]
     rest = rest[NUM_CONST + 6 :]
     consts = rest[:NUM_CONST]
-    (vs, ss, sb, e, pe, xs, ys, ts, dd, lvs, zs, rl, g1, mid, g2) = rest[NUM_CONST : NUM_CONST + 15]
-    (csem, lsem, ssem, rsem, fsem, hsem, psem, qsem, g1s, g1r, g2s, g2r) = rest[NUM_CONST + 15 :]
+    (vs, ss, sb, e, pe, xs, xc, ys, ts, dd, lvs, zs, pan_sum, rl, g1, mid, g2) = rest[
+        NUM_CONST : NUM_CONST + 17
+    ]
+    (csem, lsem, ssem, rsem, fsem, hsem, psem, qsem, g1s, g1r, g2s, g2r) = rest[NUM_CONST + 17 :]
     r = lax.axis_index("rows")
     c = lax.axis_index("band")
 
@@ -462,20 +490,39 @@
 
     rl8 = lax.rem(r, 8)
     base = r - rl8
-    q = base + c
     barrier = pltpu.get_barrier_semaphore()
 
     def greet(row, block):
         pl.semaphore_signal(barrier, inc=1, device_id=(row, block), device_id_type=MESH)
 
-    first = [(base + lax.rem(rl8 + k, 8), c) for k in range(1, 8)]
-    second = []
-    for k in range(1, 16):
-        q2 = lax.rem(q + k, 16)
-        c2 = lax.rem(q2, 8)
-        second.append((q2 - c2 + rl8, c2))
+    core = lax.rem(rl8, 2)
+    x = lax.div(rl8, 2)
+    y_hi, z = lax.div(c, 4), lax.rem(c, 4)
+    y_lo = lax.div(r, 8)
+    y = 2 * y_hi + y_lo
+
+    def step_one(dx, dcore):
+        return 2 * lax.rem(x + dx, 4) + lax.rem(core + dcore, 2)
+
+    def step_two(dy, dz):
+        return 4 * lax.rem(y + dy, 4) + lax.rem(z + dz, 4)
+
+    def place_two(slot):
+        y2 = lax.div(slot, 4)
+        return 8 * lax.rem(y2, 2) + rl8, 4 * lax.div(y2, 2) + lax.rem(slot, 4)
+
+    near = lambda d: min(d, 4 - d)
+    ones = sorted(
+        [(dx, dc) for dx in range(4) for dc in range(2) if dx or dc], key=lambda d: (-near(d[0]), -d[1])
+    )
+    twos = sorted(
+        [(dy, dz) for dy in range(4) for dz in range(4) if dy or dz],
+        key=lambda d: (-near(d[0]) - near(d[1]), d),
+    )
+    first = [(base + step_one(*d), c) for d in ones]
+    second = [place_two(step_two(*d)) for d in twos]
     around = [(lax.rem(r + 1, STRIPS), c), (lax.rem(r + STRIPS - 1, STRIPS), c)]
-    partners = first + second + around
+    partners = second + first + around
     for row, block in partners:
         greet(row, block)
 
@@ -489,8 +536,6 @@
     const_loads = [
         pltpu.make_async_copy(hbm_consts[k], consts[k], csem.at[k]) for k in range(NUM_CONST)
     ]
-    for copy in const_loads:
-        copy.start()
 
     @pl.when(r == 0)
     def _():
@@ -550,23 +595,27 @@
     def band_rows(b):
         return pl.ds(pl.multiple_of(b * 8, 8), 8)
 
+    turns = [(0, 0), (1, 2), (1, 1), (1, 3), (1, 0), (0, 2), (0, 1), (0, 3)]
+
+    def band_at(dyh, dz):
+        return 4 * lax.rem(y_hi + dyh, 2) + lax.rem(z + dz, 4)
+
     def block_send(k):
-        block = lax.rem(c + k, 8)
+        block = band_at(*turns[k])
         return remote(sb.at[block], e.at[1, pl.ds(0, 6), band_rows(c)], ssem.at[k], rsem.at[k], r, block)
 
     def block_recv(k):
-        b = lax.rem(c + 8 - k, 8)
+        b = band_at(turns[k][0], 4 - turns[k][1])
         return remote(sb.at[0], e.at[1, pl.ds(0, 6), band_rows(b)], ssem.at[k], rsem.at[k], r, c)
 
     def forward(k, side):
-        b = lax.rem(c + 8 - k, 8)
+        b = band_at(turns[k][0], 4 - turns[k][1])
         dst = e.at[2 * side, pl.ds(0, 6), band_rows(b)]
         src = sb.at[c] if k == 0 else e.at[1, pl.ds(0, 6), band_rows(b)]
         row = r + 1 if side == 0 else r - 1
         return remote(src, dst, fsem.at[side, k], hsem.at[side, k], row, c)
 
-    order = (4, 3, 5, 2, 6, 1, 7)
-    for k in order:
+    for k in range(1, 8):
         block_send(k).start()
     own = pltpu.make_async_copy(sb.at[c], e.at[1, pl.ds(0, 6), band_rows(c)], lsem.at[3])
     own.start()
@@ -575,11 +624,14 @@
     when(has_below, lambda: pan_rows(0).start())
     when(has_above, lambda: pan_rows(1).start())
 
+    for copy in const_loads:
+        copy.start()
+
     when(has_left, lambda: pan_cols(0).wait_recv())
     when(has_right, lambda: pan_cols(1).wait_recv())
     when(has_below, lambda: pan_corner(0).start())
     when(has_above, lambda: pan_corner(1).start())
-    for k in (1, 7, 2, 6, 3, 5, 4):
+    for k in range(7, 0, -1):
         block_recv(k).wait_recv()
         when(has_below, functools.partial(lambda k: forward(k, 0).start(), k))
         when(has_above, functools.partial(lambda k: forward(k, 1).start(), k))
@@ -588,42 +640,46 @@
         copy.wait()
     when(has_above, lambda: (pan_rows(0).wait_recv(), pan_corner(0).wait_recv()))
     when(has_below, lambda: (pan_rows(1).wait_recv(), pan_corner(1).wait_recv()))
+    pan_sum[...] = early_compute(e, pe, consts, r, d_out, ts, dd, xs, xc, vl)
     for k in range(8):
         when(has_above, functools.partial(lambda k: forward(k, 0).wait_recv(), k))
         when(has_below, functools.partial(lambda k: forward(k, 1).wait_recv(), k))
 
-    front_compute(e, pe, consts, r, c, d_out, ts, dd, xs, ys, lvs, vl, swu, dl, rl)
-
-    def sum_one(k):
-        row, block = first[k - 1]
-        return remote(rl, g1.at[rl8], g1s.at[k], g1r.at[k], row, block)
-
-    def sum_one_recv(k):
-        return remote(rl, g1.at[lax.rem(rl8 + 8 - k, 8)], g1s.at[k], g1r.at[k], r, c)
-
-    def sum_two(k):
-        row, block = second[k - 1]
-        return remote(mid, g2.at[q_slot], g2s.at[k], g2r.at[k], row, block)
-
-    def sum_two_recv(k):
-        return remote(mid, g2.at[lax.rem(q_slot + 16 - k, 16)], g2s.at[k], g2r.at[k], r, c)
-
-    q_slot = q
-    for k in range(1, 8):
-        sum_one(k).start()
+    front_compute(e, consts, pan_sum, r, c, ts, dd, xs, xc, ys, lvs, vl, swu, dl, rl)
+
+    me_two = 4 * y + z
+
+    def sum_one(n):
+        row, block = first[n]
+        return remote(rl, g1.at[rl8], g1s.at[n], g1r.at[n], row, block)
+
+    def sum_one_recv(n):
+        dx, dc = ones[n]
+        return remote(rl, g1.at[step_one(4 - dx, 2 - dc)], g1s.at[n], g1r.at[n], r, c)
+
+    def sum_two(n):
+        row, block = second[n]
+        return remote(mid, g2.at[me_two], g2s.at[n], g2r.at[n], row, block)
+
+    def sum_two_recv(n):
+        dy, dz = twos[n]
+        return remote(mid, g2.at[step_two(4 - dy, 4 - dz)], g2s.at[n], g2r.at[n], r, c)
+
+    for n in range(7):
+        sum_one(n).start()
     g1[rl8] = rl[...]
-    for k in range(1, 8):
-        sum_one_recv(k).wait_recv()
+    for n in range(7):
+        sum_one_recv(n).wait_recv()
     total = g1[0]
     for k in range(1, 8):
         total = total + g1[k]
     mid[...] = total
-    for k in range(1, 16):
-        sum_two(k).start()
-    g2[q_slot] = total
+    for n in range(15):
+        sum_two(n).start()
+    g2[me_two] = total
     upsample(xs, consts, zs, up_out)
-    for k in range(1, 16):
-        sum_two_recv(k).wait_recv()
+    for n in range(15):
+        sum_two_recv(n).wait_recv()
     total = g2[0]
     for k in range(1, 16):
         total = total + g2[k]
@@ -631,9 +687,9 @@
 
     for k in range(1, 8):
         block_send(k).wait_send()
-        sum_one(k).wait_send()
-    for k in range(1, 16):
-        sum_two(k).wait_send()
+        sum_one(k - 1).wait_send()
+    for n in range(15):
+        sum_two(n).wait_send()
     when(has_right, lambda: pan_cols(0).wait_send())
     when(has_left, lambda: pan_cols(1).wait_send())
     for side, cond in ((0, has_below), (1, has_above)):
@@ -665,10 +721,12 @@
             VM((112, 1792), F32),
             VM((28, 8, 512), F32),
             VM((16, 8, 512), F32),
+            VM((16, 8, 512), F32),
             VM((16, 512), F32),
             VM((24, 512), F32),
             VM((12, 8, 384), F32),
             VM((4, 384, 128), F32),
+            VM((8, 128), F32),
             VM((8, 128), F32),
             VM((8, 8, 128), F32),
             VM((8, 128), F32),
@@ -722,21 +780,28 @@
     return total
 
 
-def solve(rt, cb):
-    for k in range(38):
-        if k < 11 or k >= 16:
-            cb[k] = jnp.broadcast_to(rt[:, k : k + 1], (8, 128))
+def solve_first(rt, cb):
+    for k in range(11):
+        cb[k] = jnp.broadcast_to(rt[:, k : k + 1], (8, 128))
+    mean = [cb[9, i : i + 1, :] * (1.0 / N1) for i in range(8)]
+    mean_p = jnp.sum(cb[10], axis=0, keepdims=True) * (1.0 / N1)
+    a = [
+        [cb[j, i : i + 1, :] * (1.0 / N1) - mean[i] * mean[j] for j in range(i + 1)]
+        for i in range(8)
+    ]
+    b = [cb[8, i : i + 1, :] * (1.0 / N1) - mean[i] * mean_p for i in range(8)]
+    w = solve_spd(a, b)
+    scale = 1.0 / total_of([b[i] * w[i] for i in range(8)])
+    return [b[i] * scale for i in range(8)]
+
+
+def solve_second(rt, cb, gain):
+    for k in range(16, 38):
+        cb[k] = jnp.broadcast_to(rt[:, k : k + 1], (8, 128))
 
     def at(k, i):
         return cb[k, i : i + 1, :]
 
-    mean = [at(9, i) * (1.0 / N1) for i in range(8)]
-    mean_p = jnp.sum(cb[10], axis=0, keepdims=True) * (1.0 / N1)
-    a = [[at(j, i) * (1.0 / N1) - mean[i] * mean[j] for j in range(i + 1)] for i in range(8)]
-    b = [at(8, i) * (1.0 / N1) - mean[i] * mean_p for i in range(8)]
-    w = solve_spd(a, b)
-    scale = 1.0 / total_of([b[i] * w[i] for i in range(8)])
-    gain = [b[i] * scale for i in range(8)]
     sum_d = at(36, 0)
     sum_dd = at(37, 0)
     q = [at(32, i) for i in range(8)]
@@ -756,7 +821,7 @@
     y = [jnp.sum(cross[i], axis=0, keepdims=True) * 0.125 for i in range(8)]
     v = solve_spd(a2, y)
     share = total_of([v[i] * cross[i] for i in range(8)]) / total_of([v[i] * y[i] for i in range(8)])
-    return gain, v, share
+    return v, share
 
 
 def wide(x, copies):
@@ -764,7 +829,7 @@
 
 
 def back_kernel(rt, up, d, vl, swu, dl, joined, joined_swir, cb, gs, out, sem):
-    gain, v, share = solve(rt, cb)
+    gain = solve_first(rt, cb)
     for b in range(8):
         gs[b] = jnp.broadcast_to(gain[b], (8, 128))
 
@@ -780,6 +845,8 @@
                 )
         pltpu.make_async_copy(out.at[b], joined.at[b], sem.at[b]).start()
 
+    gain = [gs[b, 0:1, :] for b in range(8)]
+    v, share = solve_second(rt, cb, gain)
     row8 = lax.broadcasted_iota(jnp.int32, (8, 128), 0)
     v8 = jnp.zeros((8, 128), F32)
     for b in range(8):

time: 35.5 us -> 33.5 us (0.944)
  Pallas kernels: 34.7 us -> 32.7 us
    pallas_call x1, Pallas kernels: 32.2 us -> 30.4 us  [front(): pl.pallas_call(front_kernel, name='front', out_shape=[VM((8, 128), F32),...]
where the time goes in v2:
time: 33.5 us; the launch traced here: 33.4 us
  Pallas kernels  32.7 us (98%)
  between operations  0.64 us (2%)
    pallas_call x1, Pallas kernels, front(): pl.pallas_call(front_kernel, name='front', out_shape=[VM((8, 128), F32),...  30.4 us
    pallas_call x1, Pallas kernels, back(): pl.pallas_call(back_kernel, name='back', out_shape=[jax.ShapeDtypeStruct(...  2.34 us

profile of v2, /device:TPU:1, one launch (start us, length us, event | category | flops | bytes accessed | tf_op | source)
XLA Modules:
  0.0 33.4 jit_solution(10957300566871347557)
XLA Ops:
  0.6 30.4 %front.1 = (f32[8,128]{1,0:T(8,128)S(1)}, f32[384,1536]{1,0:T(8,128)S(1)}, f32[48,1536]{1,0:T(8,128)S(1)}, f32[12,8,384]{2,1,0:T(8,128)S(1)}, f32[96,384]{1,0:T(8,128)S(1)}, /*index=5*/f32[12,384]{1,0:T(8,128)S(1)}) custom-call(f32[48,1536]{1,0:T(8,128)} %pan.1, f32[288,128]{1,0:T(8,128)} %bitcast.2, f32[1,4,1024]{2,1,0:T(4,128)} %swir.1, ...), custom_call_target="tpu_custom_call" | custom-call | tf_op jit(solution)/shard_map/front/pallas_call | solution.py:702
  31.0 2.3 %back.1 = (f32[8,48,1536]{2,1,0:T(8,128)}, f32[12,8,384]{2,1,0:T(8,128)}) custom-call(f32[8,128]{1,0:T(8,128)S(1)} %get-tuple-element.10.rt, f32[384,1536]{1,0:T(8,128)S(1)} %get-tuple-element.11.up, f32[48,1536]{1,0:T(8,128)S(1)} %get-tuple-element.12.d, f32[12,8,384]{2,1,0:T(8,128)S(1)} %get-tuple-element.13.vl, f32[96,384]{1,0:T(8,128)S(1)} %get-tuple-element.14.swu, ...), custom_call_target="tpu_custom_call" | custom-call | tf_op jit(solution)/shard_map/back/pallas_call | solution.py:867

commit v3 on v2

--- a/solution.py
+++ b/solution.py
@@ -86,38 +86,15 @@
     lanes[9] = up_cols.sum(axis=0)
     row_sum = up_rows.sum(axis=0)
 
-    low = np.zeros((96, 112))
-    for f in range(96):
-        for t in range(17):
-            low[f, f + t] = G4[t]
-    mean = np.zeros((24, 112))
-    mean_low = np.zeros((24, 112))
-    for i in range(24):
+    low = np.zeros((48, 64))
+    mean = np.zeros((16, 64))
+    for f in range(48):
+        low[f, f : f + 17] = G4
+    for i in range(12):
         mean[i, 8 + 4 * i : 12 + 4 * i] = 0.25
-        mean_low[i] = low[4 * i : 4 * i + 4].mean(axis=0)
-    g3_rows = np.zeros((12, 24))
-    for i in range(12):
-        g3_rows[i, i : i + 13] = G3
-    row_stack = []
-    for variant in range(3):
-        keep = np.ones((24, 1))
-        if variant == 0:
-            keep[:6] = 0.0
-        if variant == 2:
-            keep[18:] = 0.0
-        row_stack.append(
-            np.concatenate(
-                [
-                    low[24:72],
-                    up_rows.T @ low[24:72],
-                    mean_low[6:18],
-                    g3_rows @ (keep * mean_low),
-                    mean[6:18],
-                    g3_rows @ (keep * mean),
-                ]
-            )
-        )
-    rows_hi, rows_lo = split(np.stack(row_stack))
+    mean_low = np.zeros((16, 64))
+    mean_low[:12] = low.reshape(12, 4, 64).mean(axis=1)
+    rows_hi, rows_lo = split(np.concatenate([low, up_rows.T @ low, mean_low, mean]))
 
     low_cols = np.zeros((256, 128))
     for o in range(128):
@@ -200,10 +177,12 @@
 def col_filter(x, taps):
     radius = len(taps) // 2
     total = float(taps[radius]) * x
-    for t in range(-radius, radius + 1):
-        if t:
-            total = total + float(taps[t + radius]) * shifted(x, t)
+    for t in range(1, radius + 1):
+        total = total + float(taps[radius + t]) * (shifted(x, t) + shifted(x, -t))
     return total
+
+
+TILES = 7
 
 
 def pick(e, strip, row, tile):
@@ -211,23 +190,26 @@
 
 
 def vnir_row(e, strip, i):
-    if i < 8:
-        parts = [pick(e, strip, i, t) for t in range(3)] + [pick(e, strip, i, 5)]
-    else:
-        j = i - 8
-        parts = [
-            pick(e, strip, j, 3),
-            pick(e, strip, 4 + j, 3),
-            pick(e, strip, j, 4),
-            pltpu.roll(pick(e, strip, j, 5), 64, 1),
-        ]
-    return jnp.concatenate(parts, axis=1)
+    first, at = (0, i) if strip == 2 or (strip == 1 and i < 8) else (4, i - 4)
+    halo = pick(e, strip, i, 3) if i < 8 else pltpu.roll(pick(e, strip, i - 8, 3), 64, 1)
+    return jnp.concatenate([pick(e, strip, at, first + t) for t in range(3)] + [halo], axis=1)
 
 
 def swir_row(e, strip, j):
-    return jnp.concatenate(
-        [pick(e, strip, 4 + j, 4), pltpu.roll(pick(e, strip, 4 + j, 5), 64, 1)], axis=1
-    )
+    at = lane((8, 128))
+    base = 16 if j < 2 else 80
+    row = None
+    for k in range(4):
+        part = pltpu.roll(pick(e, strip, 4 * (j % 2) + k, 3), (32 * k - base) % 128, 1)
+        row = part if row is None else jnp.where(at >= 32 * k, part, row)
+    return jnp.concatenate([row, pltpu.roll(pick(e, strip, 4 + j, 3), 64, 1)], axis=1)
+
+
+def total_of(values):
+    total = values[0]
+    for value in values[1:]:
+        total = total + value
+    return total
 
 
 def fold(x):
@@ -247,29 +229,38 @@
     def short(tile):
         return ss[0:4, 128 * tile : 128 * tile + 128] if 0 <= tile < 8 else zero[0:4]
 
+    sub = lax.broadcasted_iota(jnp.int32, (8, 128), 0)
     for d in range(BLOCKS):
         for t in range(3):
             sb[d, t] = coarse(0, 3 * d + t)
-        sb[d, 3, 0:4] = coarse(8, 3 * d)[0:4]
-        sb[d, 3, 4:8] = coarse(8, 3 * d + 1)[0:4]
-        sb[d, 4, 0:4] = coarse(8, 3 * d + 2)[0:4]
-        sb[d, 4, 4:8] = short(d)
-        sb[d, 5, 0:4] = edge(coarse(8, 3 * d + 3), coarse(8, 3 * d - 1))[0:4]
-        sb[d, 5, 4:8] = edge(short(d + 1), short(d - 1))
-        other = pltpu.roll(sb[d, 5], 64, 1)
+            sb[d, 4 + t] = coarse(4, 3 * d + t)
+        sb[d, 3, 0:4] = edge(coarse(8, 3 * d + 3), coarse(8, 3 * d - 1))[0:4]
+        sb[d, 3, 4:8] = edge(short(d + 1), short(d - 1))
+        other = pltpu.roll(sb[d, 3], 64, 1)
         own = edge(coarse(0, 3 * d + 3), coarse(0, 3 * d - 1))
-        sb[d, 5] = jnp.where((at >= 32) & (at < 96), other, own)
-
-
-def pan_stage(pan_ext, consts, variant, d_out, ts, dd):
-    rows_hi, rows_lo, low_hi, low_lo, mean_c, back_hi, back_lo = consts[:7]
+        tile = jnp.where((at >= 56) & (at < 72), other, own)
+        for j in (0, 2):
+            base = 16 + 32 * j
+            rows = jnp.where(
+                sub < 4,
+                ss[j : j + 1, 128 * d : 128 * d + 128],
+                ss[j + 1 : j + 2, 128 * d : 128 * d + 128],
+            )
+            quarters = None
+            for k in range(4):
+                part = pltpu.roll(rows, (base - 32 * k) % 128, 1)
+                quarters = part if quarters is None else jnp.where(lax.rem(sub, 4) == k, part, quarters)
+            tile = jnp.where((at >= base) & (at < base + 32), quarters, tile)
+        sb[d, 3] = tile
+
+
+def pan_full(pan_ext):
     halo = edge(pan_ext[:, 1664:1792], pan_ext[:, 1536:1664])
-    full = jnp.concatenate([pan_ext[:, 0:1536], halo], axis=1)
-    fh, fl = halves(full)
-    rh, rl = rows_hi[variant], rows_lo[variant]
-    q = mm(rh, fh) + mm(rh, fl) + mm(rl, fh)
-    top = q[0:88]
-    tiles = [top[:, 128 * j : 128 * j + 128] for j in range(13)]
+    return halves(jnp.concatenate([pan_ext[:, 0:1536], halo], axis=1))
+
+
+def pan_low_tiles(rows, consts, count):
+    tiles = [rows[:count, 128 * j : 128 * j + 128] for j in range(13)]
     lhs = jnp.concatenate(
         [
             jnp.concatenate([tiles[j], edge(tiles[(j + 1) % 13], tiles[(j + 12) % 13])], axis=1)
@@ -277,12 +268,37 @@
         ],
         axis=0,
     )
-    low = dot3(lhs, low_hi[...], low_lo[...])
-    low_tile = [low[88 * j : 88 * j + 88] for j in range(13)]
+    low = dot3(lhs, consts[2][...], consts[3][...])
+    return [low[count * j : count * j + count] for j in range(13)]
+
+
+def mean_stage(pan_ext, consts, dd, down):
+    fh, fl = pan_full(pan_ext)
+    rh, rl = consts[0][64:96], consts[1][64:96]
+    q = mm(rh, fh) + mm(rh, fl) + mm(rl, fh)
+    low_tile = pan_low_tiles(q, consts, 16)
+    diff = [q[16:32, 128 * j : 128 * j + 128] - low_tile[j] for j in range(13)]
+    lhs = jnp.concatenate(
+        [jnp.concatenate(diff[4 * t : 4 * t + 4], axis=1) for t in range(3)], axis=0
+    )
+    mean_c = consts[4]
+    main = dot2(lhs, mean_c[0:512])
+    for t in range(3):
+        dd[8:24, 128 * t : 128 * t + 128] = main[16 * t : 16 * t + 16]
+    dd[8:24, 384:512] = dot2(diff[12], mean_c[512:640])
+    down[...] = dd[12:20, :]
+
+
+def pan_stage(pan_ext, consts, d_out, ts):
+    back_hi, back_lo = consts[5:7]
+    fh, fl = pan_full(pan_ext)
+    rh, rl = consts[0][0:64], consts[1][0:64]
+    q = mm(rh, fh) + mm(rh, fl) + mm(rl, fh)
+    low_tile = pan_low_tiles(q, consts, 64)
     total = jnp.zeros((8, 128), F32)
     for j in range(12):
         d_out[:, 128 * j : 128 * j + 128] = (
-            pan_ext[32:80, 128 * j : 128 * j + 128] - low_tile[j][0:48]
+            pan_ext[8:56, 128 * j : 128 * j + 128] - low_tile[j][0:48]
         )
         for k in range(6):
             total = total + low_tile[j][8 * k : 8 * k + 8]
@@ -302,14 +318,6 @@
     for t in range(3):
         ts[:, 128 * t : 128 * t + 128] = main[16 * t : 16 * t + 16]
     ts[:, 384:512] = rim
-    diff = [q[88:112, 128 * j : 128 * j + 128] - low_tile[j][64:88] for j in range(13)]
-    lhs = jnp.concatenate(
-        [jnp.concatenate(diff[4 * t : 4 * t + 4], axis=1) for t in range(3)], axis=0
-    )
-    main = dot2(lhs, mean_c[0:512])
-    for t in range(3):
-        dd[0:24, 128 * t : 128 * t + 128] = main[24 * t : 24 * t + 24]
-    dd[0:24, 384:512] = dot2(diff[12], mean_c[512:640])
     return total
 
 
@@ -336,71 +344,85 @@
     return y
 
 
-def early_compute(e, pan_ext, consts, r, d_out, ts, dd, xs, xc, vl):
+OWN = range(2, 14)
+RIM = (0, 1, 14, 15)
+EARLY = range(2, 10)
+
+
+def gram_row(xc, i, among, scale):
+    total = None
+    for j in among:
+        if GRAM_ROWS[i, j] != 0.0:
+            term = float(scale * GRAM_ROWS[i, j]) * xc[j]
+            total = term if total is None else total + term
+    return total
+
+
+def add_products(acc, xs, ys, ts, ones, i):
+    x = xs[i + 6]
+    for j in range(8):
+        acc[j] = acc[j] + fold(x * ys[i, j : j + 1, :])
+    acc[8] = acc[8] + fold(x * ts[i : i + 1, :])
+    acc[9] = acc[9] + float(ROW_SUM[i]) * fold(x * ones)
+
+
+def early_compute(e, consts, ts, xs, xc, ys, vl, lvp, sums):
     lanes = consts[11]
-    variant = jnp.where(r == 0, 0, jnp.where(r == STRIPS - 1, 2, 1))
     for i in range(12):
         row = vnir_row(e, 1, i)
         xs[i + 8] = row
         xc[i + 2] = gram_cols(lanes, row)
-    for i in range(2, 10):
-        vl[i] = col_filter(mean_row(xs, i + 6), MEAN_TAPS)[:, 0:384]
-    return pan_stage(pan_ext, consts, variant, d_out, ts, dd)
-
-
-def front_compute(e, consts, pan_sum, r, c, ts, dd, xs, xc, ys, lvs, vl, swu, dl, rl):
+    acc = [jnp.zeros((8, 128), F32) for _ in range(10)]
+    for i in OWN:
+        ys[i] = gram_row(xc, i, OWN, 1.0)
+    for i in OWN:
+        add_products(acc, xs, ys, ts, lanes[9:10, :], i)
+    for k in range(10):
+        sums[k] = acc[k]
+    means = {i: mean_row(xs, i + 6) for i in EARLY}
+    for i in EARLY:
+        vl[i] = col_filter(means[i], MEAN_TAPS)[:, 0:384]
+    for i in range(12):
+        lvp[i] = total_of([float(G3[k - i + 6]) * means[k] for k in EARLY if abs(k - i) <= 6])
+
+
+def front_compute(e, consts, sums_ref, r, c, ts, dd, xs, xc, ys, lvs, vl, lvp, swu, dl, rl):
     third_hi, third_lo, lanes = consts[9:12]
-    sums = {10: pan_sum[...]}
     for k in range(28):
         if k < 8:
             xs[k] = vnir_row(e, 0, k + 4)
         elif k >= 20:
             xs[k] = vnir_row(e, 2, k - 20)
-    for i in (0, 1, 14, 15):
-        xc[i] = gram_cols(lanes, xs[i + 6])
-    for i in range(16):
-        total = None
-        for j in range(16):
-            if GRAM_ROWS[i, j] != 0.0:
-                term = float(GRAM_ROWS[i, j]) * xc[j]
-                total = term if total is None else total + term
-        ys[i] = total
-    acc = [jnp.zeros((8, 128), F32) for _ in range(10)]
-    ones = lanes[9:10, :]
-    for i in range(16):
-        x = xs[i + 6]
-        for j in range(8):
-            acc[j] = acc[j] + fold(x * ys[i, j : j + 1, :])
-        acc[8] = acc[8] + fold(x * ts[i : i + 1, :])
-        acc[9] = acc[9] + float(ROW_SUM[i]) * fold(x * ones)
-    for k in range(10):
-        sums[k] = acc[k]
     up_keep = jnp.where(r == 0, 0.0, 1.0)
     down_keep = jnp.where(r == STRIPS - 1, 0.0, 1.0)
     mask = column_mask(c)
-    mean_rows = []
-    for i in range(24):
-        total = mean_row(xs, i)
-        if i < 6:
-            total = total * up_keep
-        if i >= 18:
-            total = total * down_keep
-        mean_rows.append(total)
+    means = {}
+    for i in range(-6, 18):
+        if i not in EARLY:
+            row = mean_row(xs, i + 6)
+            means[i] = row * up_keep if i < 0 else (row * down_keep if i >= 12 else row)
     for i in range(12):
-        total = float(G3[6]) * mean_rows[i + 6]
-        for t in range(6):
-            total = total + float(G3[t]) * (mean_rows[i + t] + mean_rows[i + 12 - t])
+        total = lvp[i] + total_of(
+            [float(G3[k - i + 6]) * means[k] for k in means if abs(k - i) <= 6]
+        )
         lowered = col_filter(total, MEAN_TAPS) * mask
         lowered = col_filter(lowered, G3)[:, 0:384]
         lvs[i] = lowered
-        if 2 <= i < 10:
+        if i in EARLY:
             vl[i] = vl[i] - lowered
         else:
-            vl[i] = col_filter(mean_rows[i + 6], MEAN_TAPS)[:, 0:384] - lowered
-    dcol = dd[8:24, :] * mask
-    dcol = col_filter(dcol, G3)[:, 0:384]
-    low_d = dcol[4:16]
-    dl[...] = dd[0:12, 0:384] - low_d
+            vl[i] = col_filter(means[i], MEAN_TAPS)[:, 0:384] - lowered
+    for i in RIM:
+        xc[i] = gram_cols(lanes, xs[i + 6])
+    acc = [sums_ref[k] for k in range(10)]
+    for i in RIM:
+        ys[i] = gram_row(xc, i, OWN, 2.0) + gram_row(xc, i, RIM, 1.0)
+        add_products(acc, xs, ys, ts, lanes[9:10, :], i)
+    sums = {k: acc[k] for k in range(10)}
+    sums[10] = sums_ref[10]
+    dcol = total_of([float(G3[t]) * dd[t + 2 : t + 14, :] for t in range(13)]) * mask
+    low_d = col_filter(dcol, G3)[:, 0:384]
+    dl[...] = dd[8:20, 0:384] - low_d
     ts[0:12, 0:384] = low_d
     srow = [
         swir_row(e, *at)
@@ -475,10 +497,10 @@
     rt, up_out, d_out, vl, swu, dl = rest[NUM_CONST : NUM_CONST + 6]
     rest = rest[NUM_CONST + 6 :]
     consts = rest[:NUM_CONST]
-    (vs, ss, sb, e, pe, xs, xc, ys, ts, dd, lvs, zs, pan_sum, rl, g1, mid, g2) = rest[
-        NUM_CONST : NUM_CONST + 17
+    (vs, ss, sb, e, pe, xs, xc, ys, ts, dd, lvs, zs, sums, rl, g1, mid, g2, lvp, down, dup, ddn) = rest[
+        NUM_CONST : NUM_CONST + 21
     ]
-    (csem, lsem, ssem, rsem, fsem, hsem, psem, qsem, g1s, g1r, g2s, g2r) = rest[NUM_CONST + 17 :]
+    (csem, lsem, ssem, rsem, fsem, hsem, psem, qsem, g1s, g1r, g2s, g2r) = rest[NUM_CONST + 21 :]
     r = lax.axis_index("rows")
     c = lax.axis_index("band")
 
@@ -521,15 +543,21 @@
     )
     first = [(base + step_one(*d), c) for d in ones]
     second = [place_two(step_two(*d)) for d in twos]
-    around = [(lax.rem(r + 1, STRIPS), c), (lax.rem(r + STRIPS - 1, STRIPS), c)]
-    partners = second + first + around
-    for row, block in partners:
+    strips = ((1, r < STRIPS - 1), (-1, r > 0))
+    beside = [(r + dr, c, ok) for dr, ok in strips]
+    greetings = len(second) + len(first)
+    for row, block in second:
+        greet(row, block)
+    for row, block, ok in beside:
+        pl.when(ok)(functools.partial(greet, row, block))
+        greetings = greetings + jnp.where(ok, 1, 0)
+    for row, block in first:
         greet(row, block)
 
     loads = [
         pltpu.make_async_copy(vnir, vs.at[pl.ds(0, 288)], lsem.at[0]),
         pltpu.make_async_copy(swir.at[0], ss, lsem.at[1]),
-        pltpu.make_async_copy(pan, pe.at[pl.ds(32, 48), pl.ds(0, 1536)], lsem.at[2]),
+        pltpu.make_async_copy(pan, pe.at[pl.ds(8, 48), pl.ds(0, 1536)], lsem.at[2]),
     ]
     for copy in loads:
         copy.start()
@@ -539,47 +567,54 @@
 
     @pl.when(r == 0)
     def _():
-        pe[0:32, :] = jnp.zeros((32, 1792), F32)
-        e[0] = jnp.zeros((6, 64, 128), F32)
+        pe[0:8, :] = jnp.zeros((8, 1792), F32)
+        e[0, 3:7] = jnp.zeros((4, 64, 128), F32)
+        dup[...] = jnp.zeros((8, 512), F32)
 
     @pl.when(r == STRIPS - 1)
     def _():
-        pe[80:112, :] = jnp.zeros((32, 1792), F32)
-        e[2] = jnp.zeros((6, 64, 128), F32)
+        pe[56:64, :] = jnp.zeros((8, 1792), F32)
+        e[2, 0:4] = jnp.zeros((4, 64, 128), F32)
+        ddn[...] = jnp.zeros((8, 512), F32)
 
     @pl.when(c == 0)
     def _():
-        pe[32:80, 1536:1664] = jnp.zeros((48, 128), F32)
+        pe[8:56, 1536:1664] = jnp.zeros((48, 128), F32)
 
     @pl.when(c == BLOCKS - 1)
     def _():
-        pe[32:80, 1664:1792] = jnp.zeros((48, 128), F32)
+        pe[8:56, 1664:1792] = jnp.zeros((48, 128), F32)
 
     loads[0].wait()
     loads[1].wait()
     pack(vs, ss, sb)
     loads[2].wait()
-    pl.semaphore_wait(barrier, len(partners))
+    pl.semaphore_wait(barrier, greetings)
 
     def pan_cols(side):
-        src = pe.at[pl.ds(32, 48), pl.ds(1408, 128)] if side == 0 else pan_first
-        dst = pe.at[pl.ds(32, 48), pl.ds(1536 + 128 * side, 128)]
+        src = pe.at[pl.ds(8, 48), pl.ds(1408, 128)] if side == 0 else pan_first
+        dst = pe.at[pl.ds(8, 48), pl.ds(1536 + 128 * side, 128)]
         block = c + 1 if side == 0 else c - 1
         return remote(src, dst, psem.at[side], qsem.at[side], r, block)
 
-    pan_first = pe.at[pl.ds(32, 48), pl.ds(0, 128)]
+    pan_first = pe.at[pl.ds(8, 48), pl.ds(0, 128)]
+
+    def pan_part(side, cols, n):
+        src = pe.at[pl.ds(48, 8), cols] if side == 0 else pe.at[pl.ds(8, 8), cols]
+        dst = pe.at[pl.ds(0, 8), cols] if side == 0 else pe.at[pl.ds(56, 8), cols]
+        row = r + 1 if side == 0 else r - 1
+        return remote(src, dst, psem.at[n + side], qsem.at[n + side], row, c)
 
     def pan_rows(side):
-        src = pe.at[pl.ds(48, 32), pl.ds(0, 1536)] if side == 0 else pe.at[pl.ds(32, 32), pl.ds(0, 1536)]
-        dst = pe.at[pl.ds(0, 32), pl.ds(0, 1536)] if side == 0 else pe.at[pl.ds(80, 32), pl.ds(0, 1536)]
+        return pan_part(side, pl.ds(0, 1536), 2)
+
+    def pan_corner(side):
+        return pan_part(side, pl.ds(1536, 256), 4)
+
+    def mean_rows(side):
+        src, dst = (down, dup) if side == 0 else (dd.at[pl.ds(8, 8)], ddn)
         row = r + 1 if side == 0 else r - 1
-        return remote(src, dst, psem.at[2 + side], qsem.at[2 + side], row, c)
-
-    def pan_corner(side):
-        src = pe.at[pl.ds(48, 32), pl.ds(1536, 256)] if side == 0 else pe.at[pl.ds(32, 32), pl.ds(1536, 256)]
-        dst = pe.at[pl.ds(0, 32), pl.ds(1536, 256)] if side == 0 else pe.at[pl.ds(80, 32), pl.ds(1536, 256)]
-        row = r + 1 if side == 0 else r - 1
-        return remote(src, dst, psem.at[4 + side], qsem.at[4 + side], row, c)
+        return remote(src, dst, psem.at[6 + side], qsem.at[6 + side], row, c)
 
     has_below, has_above = r < STRIPS - 1, r > 0
     has_right, has_left = c < BLOCKS - 1, c > 0
@@ -602,22 +637,23 @@
 
     def block_send(k):
         block = band_at(*turns[k])
-        return remote(sb.at[block], e.at[1, pl.ds(0, 6), band_rows(c)], ssem.at[k], rsem.at[k], r, block)
+        return remote(sb.at[block], e.at[1, pl.ds(0, TILES), band_rows(c)], ssem.at[k], rsem.at[k], r, block)
 
     def block_recv(k):
         b = band_at(turns[k][0], 4 - turns[k][1])
-        return remote(sb.at[0], e.at[1, pl.ds(0, 6), band_rows(b)], ssem.at[k], rsem.at[k], r, c)
+        return remote(sb.at[0], e.at[1, pl.ds(0, TILES), band_rows(b)], ssem.at[k], rsem.at[k], r, c)
 
     def forward(k, side):
         b = band_at(turns[k][0], 4 - turns[k][1])
-        dst = e.at[2 * side, pl.ds(0, 6), band_rows(b)]
-        src = sb.at[c] if k == 0 else e.at[1, pl.ds(0, 6), band_rows(b)]
+        part = pl.ds(3 - 3 * side, 4)
+        dst = e.at[2 * side, part, band_rows(b)]
+        src = sb.at[c, part] if k == 0 else e.at[1, part, band_rows(b)]
         row = r + 1 if side == 0 else r - 1
         return remote(src, dst, fsem.at[side, k], hsem.at[side, k], row, c)
 
     for k in range(1, 8):
         block_send(k).start()
-    own = pltpu.make_async_copy(sb.at[c], e.at[1, pl.ds(0, 6), band_rows(c)], lsem.at[3])
+    own = pltpu.make_async_copy(sb.at[c], e.at[1, pl.ds(0, TILES), band_rows(c)], lsem.at[3])
     own.start()
     when(has_below, lambda: forward(0, 0).start())
     when(has_above, lambda: forward(0, 1).start())
@@ -640,12 +676,20 @@
         copy.wait()
     when(has_above, lambda: (pan_rows(0).wait_recv(), pan_corner(0).wait_recv()))
     when(has_below, lambda: (pan_rows(1).wait_recv(), pan_corner(1).wait_recv()))
-    pan_sum[...] = early_compute(e, pe, consts, r, d_out, ts, dd, xs, xc, vl)
+    mean_stage(pe, consts, dd, down)
+    when(has_below, lambda: mean_rows(0).start())
+    when(has_above, lambda: mean_rows(1).start())
+    sums[10] = pan_stage(pe, consts, d_out, ts)
+    early_compute(e, consts, ts, xs, xc, ys, vl, lvp, sums)
     for k in range(8):
         when(has_above, functools.partial(lambda k: forward(k, 0).wait_recv(), k))
         when(has_below, functools.partial(lambda k: forward(k, 1).wait_recv(), k))
 
-    front_compute(e, consts, pan_sum, r, c, ts, dd, xs, xc, ys, lvs, vl, swu, dl, rl)
+    when(has_above, lambda: mean_rows(0).wait_recv())
+    when(has_below, lambda: mean_rows(1).wait_recv())
+    dd[0:8] = dup[...]
+    dd[20:28] = ddn[...]
+    front_compute(e, consts, sums, r, c, ts, dd, xs, xc, ys, lvs, vl, lvp, swu, dl, rl)
 
     me_two = 4 * y + z
 
@@ -685,6 +729,8 @@
         total = total + g2[k]
     rt[...] = total
 
+    when(has_below, lambda: mean_rows(0).wait_send())
+    when(has_above, lambda: mean_rows(1).wait_send())
     for k in range(1, 8):
         block_send(k).wait_send()
         sum_one(k - 1).wait_send()
@@ -716,29 +762,33 @@
         + [
             VM((384, 128), F32),
             VM((4, 1024), F32),
-            VM((8, 6, 8, 128), F32),
-            VM((3, 6, 64, 128), F32),
-            VM((112, 1792), F32),
+            VM((8, TILES, 8, 128), F32),
+            VM((3, TILES, 64, 128), F32),
+            VM((64, 1792), F32),
             VM((28, 8, 512), F32),
             VM((16, 8, 512), F32),
             VM((16, 8, 512), F32),
             VM((16, 512), F32),
-            VM((24, 512), F32),
+            VM((32, 512), F32),
             VM((12, 8, 384), F32),
             VM((4, 384, 128), F32),
-            VM((8, 128), F32),
+            VM((11, 8, 128), F32),
             VM((8, 128), F32),
             VM((8, 8, 128), F32),
             VM((8, 128), F32),
             VM((16, 8, 128), F32),
+            VM((12, 8, 512), F32),
+            VM((8, 512), F32),
+            VM((8, 512), F32),
+            VM((8, 512), F32),
             pltpu.SemaphoreType.DMA((NUM_CONST,)),
             pltpu.SemaphoreType.DMA((4,)),
             pltpu.SemaphoreType.DMA((8,)),
             pltpu.SemaphoreType.DMA((8,)),
             pltpu.SemaphoreType.DMA((2, 8)),
             pltpu.SemaphoreType.DMA((2, 8)),
-            pltpu.SemaphoreType.DMA((6,)),
-            pltpu.SemaphoreType.DMA((6,)),
+            pltpu.SemaphoreType.DMA((8,)),
+            pltpu.SemaphoreType.DMA((8,)),
             pltpu.SemaphoreType.DMA((8,)),
             pltpu.SemaphoreType.DMA((8,)),
             pltpu.SemaphoreType.DMA((16,)),
@@ -773,20 +823,16 @@
     return z
 
 
-def total_of(values):
-    total = values[0]
-    for value in values[1:]:
-        total = total + value
-    return total
-
-
 def solve_first(rt, cb):
     for k in range(11):
         cb[k] = jnp.broadcast_to(rt[:, k : k + 1], (8, 128))
     mean = [cb[9, i : i + 1, :] * (1.0 / N1) for i in range(8)]
     mean_p = jnp.sum(cb[10], axis=0, keepdims=True) * (1.0 / N1)
     a = [
-        [cb[j, i : i + 1, :] * (1.0 / N1) - mean[i] * mean[j] for j in range(i + 1)]
+        [
+            (cb[j, i : i + 1, :] + cb[i, j : j + 1, :]) * (0.5 / N1) - mean[i] * mean[j]
+            for j in range(i + 1)
+        ]
         for i in range(8)
     ]
     b = [cb[8, i : i + 1, :] * (1.0 / N1) - mean[i] * mean_p for i in range(8)]

time: 33.5 us -> 31.9 us (0.952)
  Pallas kernels: 32.7 us -> 31.1 us
    pallas_call x1, Pallas kernels: 30.4 us -> 28.8 us  [front(): pl.pallas_call(front_kernel, name='front', out_shape=[VM((8, 128), F32),...]
where the time goes in v3:
time: 31.9 us; the launch traced here: 31.7 us
  Pallas kernels  31.1 us (97%)
  between operations  0.64 us (2%)
    pallas_call x1, Pallas kernels, front(): pl.pallas_call(front_kernel, name='front', out_shape=[VM((8, 128), F32),...  28.8 us
    pallas_call x1, Pallas kernels, back(): pl.pallas_call(back_kernel, name='back', out_shape=[jax.ShapeDtypeStruct(...  2.34 us

profile of v3, /device:TPU:1, one launch (start us, length us, event | category | flops | bytes accessed | tf_op | source)
XLA Modules:
  0.0 31.7 jit_solution(17626858731390892986)
XLA Ops:
  0.6 28.8 %front.1 = (f32[8,128]{1,0:T(8,128)S(1)}, f32[384,1536]{1,0:T(8,128)S(1)}, f32[48,1536]{1,0:T(8,128)S(1)}, f32[12,8,384]{2,1,0:T(8,128)S(1)}, f32[96,384]{1,0:T(8,128)S(1)}, /*index=5*/f32[12,384]{1,0:T(8,128)S(1)}) custom-call(f32[48,1536]{1,0:T(8,128)} %pan.1, f32[288,128]{1,0:T(8,128)} %bitcast.2, f32[1,4,1024]{2,1,0:T(4,128)} %swir.1, ...), custom_call_target="tpu_custom_call" | custom-call | tf_op jit(solution)/shard_map/front/pallas_call | solution.py:748
  29.4 2.3 %back.1 = (f32[8,48,1536]{2,1,0:T(8,128)}, f32[12,8,384]{2,1,0:T(8,128)}) custom-call(f32[8,128]{1,0:T(8,128)S(1)} %get-tuple-element.10.rt, f32[384,1536]{1,0:T(8,128)S(1)} %get-tuple-element.11.up, f32[48,1536]{1,0:T(8,128)S(1)} %get-tuple-element.12.d, f32[12,8,384]{2,1,0:T(8,128)S(1)} %get-tuple-element.13.vl, f32[96,384]{1,0:T(8,128)S(1)} %get-tuple-element.14.swu, ...), custom_call_target="tpu_custom_call" | custom-call | tf_op jit(solution)/shard_map/back/pallas_call | solution.py:913

commit v4 on v3

--- a/solution.py
+++ b/solution.py
@@ -125,6 +125,18 @@
         for p in range(3):
             for t in range(5):
                 third[(m + t - 2) % 256, 3 * m + p] += C3[t, p]
+    both = np.convolve(MEAN_TAPS, G3)
+    joint = np.zeros((256, 128))
+    for o in range(128):
+        for t in range(-8, 9):
+            joint[(o + t) % 256, o] = both[t + 8]
+    for o in range(6):
+        for k in (-1, -2):
+            if o - k <= 6:
+                for source in range(k + 3):
+                    joint[128 + 16 + source, o] -= G3[6 + o - k] * MEAN_TAPS[2 + source - k]
+        joint[128 + 111, 127 - o] = joint[128 + 16, o]
+        joint[128 + 110, 127 - o] = joint[128 + 17, o]
     constants = (
         rows_hi,
         rows_lo,
@@ -133,6 +145,7 @@
         *split(back_cols),
         *split(fine),
         *split(third),
+        *split(joint),
         lanes,
     )
     return constants, gram_rows, row_sum, up_rows
@@ -367,7 +380,7 @@
 
 
 def early_compute(e, consts, ts, xs, xc, ys, vl, lvp, sums):
-    lanes = consts[11]
+    lanes = consts[13]
     for i in range(12):
         row = vnir_row(e, 1, i)
         xs[i + 8] = row
@@ -387,7 +400,7 @@
 
 
 def front_compute(e, consts, sums_ref, r, c, ts, dd, xs, xc, ys, lvs, vl, lvp, swu, dl, rl):
-    third_hi, third_lo, lanes = consts[9:12]
+    third_hi, third_lo, joint_hi, joint_lo, lanes = consts[9:14]
     for k in range(28):
         if k < 8:
             xs[k] = vnir_row(e, 0, k + 4)
@@ -401,17 +414,33 @@
         if i not in EARLY:
             row = mean_row(xs, i + 6)
             means[i] = row * up_keep if i < 0 else (row * down_keep if i >= 12 else row)
+    at = lane((8, 128))
+    left = (at >= 16) & (at < 18) & (c == 0)
+    right = (at >= 110) & (at < 112) & (c == BLOCKS - 1)
+    rows = []
     for i in range(12):
         total = lvp[i] + total_of(
             [float(G3[k - i + 6]) * means[k] for k in means if abs(k - i) <= 6]
         )
-        lowered = col_filter(total, MEAN_TAPS) * mask
-        lowered = col_filter(lowered, G3)[:, 0:384]
-        lvs[i] = lowered
+        rows.append(total)
+    lhs = []
+    for t in range(3):
+        for i in range(12):
+            tile = [rows[i][:, 128 * k : 128 * k + 128] for k in range(4)]
+            rim = jnp.where(at < 8, tile[t + 1], jnp.where(at >= 120, tile[(t + 3) % 4], 0.0))
+            if t == 0:
+                rim = jnp.where(left, pltpu.roll(tile[0], 16, 1), rim)
+            if t == 2:
+                rim = jnp.where(right, pltpu.roll(tile[2], 112, 1), rim)
+            lhs.append(jnp.concatenate([tile[t], rim], axis=1))
+    lowered = dot3(jnp.concatenate(lhs, axis=0), joint_hi[...], joint_lo[...])
+    for i in range(12):
+        low = jnp.concatenate([lowered[96 * t + 8 * i : 96 * t + 8 * i + 8] for t in range(3)], axis=1)
+        lvs[i] = low
         if i in EARLY:
-            vl[i] = vl[i] - lowered
+            vl[i] = vl[i] - low
         else:
-            vl[i] = col_filter(means[i], MEAN_TAPS)[:, 0:384] - lowered
+            vl[i] = col_filter(means[i], MEAN_TAPS)[:, 0:384] - low
     for i in RIM:
         xc[i] = gram_cols(lanes, xs[i + 6])
     acc = [sums_ref[k] for k in range(10)]
@@ -500,7 +529,7 @@
     (vs, ss, sb, e, pe, xs, xc, ys, ts, dd, lvs, zs, sums, rl, g1, mid, g2, lvp, down, dup, ddn) = rest[
         NUM_CONST : NUM_CONST + 21
     ]
-    (csem, lsem, ssem, rsem, fsem, hsem, psem, qsem, g1s, g1r, g2s, g2r) = rest[NUM_CONST + 21 :]
+    (csem, lsem, ssem, rsem, fsem, hsem, psem, qsem, g1s, g1r, g2s, g2r, dsem, tsem) = rest[NUM_CONST + 21 :]
     r = lax.axis_index("rows")
     c = lax.axis_index("band")
 
@@ -544,7 +573,9 @@
     first = [(base + step_one(*d), c) for d in ones]
     second = [place_two(step_two(*d)) for d in twos]
     strips = ((1, r < STRIPS - 1), (-1, r > 0))
-    beside = [(r + dr, c, ok) for dr, ok in strips]
+    blocks = ((1, c < BLOCKS - 1), (-1, c > 0))
+    beside = [(r + dr, c + dc, ok & also) for dr, ok in strips for dc, also in blocks]
+    beside += [(r + dr, c, ok) for dr, ok in strips]
     greetings = len(second) + len(first)
     for row, block in second:
         greet(row, block)
@@ -579,11 +610,11 @@
 
     @pl.when(c == 0)
     def _():
-        pe[8:56, 1536:1664] = jnp.zeros((48, 128), F32)
+        pe[:, 1536:1664] = jnp.zeros((64, 128), F32)
 
     @pl.when(c == BLOCKS - 1)
     def _():
-        pe[8:56, 1664:1792] = jnp.zeros((48, 128), F32)
+        pe[:, 1664:1792] = jnp.zeros((64, 128), F32)
 
     loads[0].wait()
     loads[1].wait()
@@ -608,8 +639,15 @@
     def pan_rows(side):
         return pan_part(side, pl.ds(0, 1536), 2)
 
-    def pan_corner(side):
-        return pan_part(side, pl.ds(1536, 256), 4)
+    def pan_corner(side, across):
+        src = pe.at[
+            pl.ds(48 if side == 0 else 8, 8), pl.ds(1408 if across == 0 else 0, 128)
+        ]
+        dst = pe.at[pl.ds(0 if side == 0 else 56, 8), pl.ds(1536 + 128 * across, 128)]
+        row = r + 1 if side == 0 else r - 1
+        block = c + 1 if across == 0 else c - 1
+        n = 2 * side + across
+        return remote(src, dst, dsem.at[n], tsem.at[n], row, block)
 
     def mean_rows(side):
         src, dst = (down, dup) if side == 0 else (dd.at[pl.ds(8, 8)], ddn)
@@ -618,6 +656,10 @@
 
     has_below, has_above = r < STRIPS - 1, r > 0
     has_right, has_left = c < BLOCKS - 1, c > 0
+    to = {(s, a): (has_below if s == 0 else has_above) & (has_right if a == 0 else has_left)
+          for s in range(2) for a in range(2)}
+    into = {(s, a): (has_above if s == 0 else has_below) & (has_left if a == 0 else has_right)
+            for s in range(2) for a in range(2)}
 
     def when(cond, action):
         @pl.when(cond)
@@ -626,6 +668,8 @@
 
     when(has_right, lambda: pan_cols(0).start())
     when(has_left, lambda: pan_cols(1).start())
+    for key in to:
+        when(to[key], functools.partial(lambda key: pan_corner(*key).start(), key))
 
     def band_rows(b):
         return pl.ds(pl.multiple_of(b * 8, 8), 8)
@@ -663,22 +707,22 @@
     for copy in const_loads:
         copy.start()
 
+    for copy in const_loads:
+        copy.wait()
     when(has_left, lambda: pan_cols(0).wait_recv())
     when(has_right, lambda: pan_cols(1).wait_recv())
-    when(has_below, lambda: pan_corner(0).start())
-    when(has_above, lambda: pan_corner(1).start())
+    when(has_above, lambda: pan_rows(0).wait_recv())
+    when(has_below, lambda: pan_rows(1).wait_recv())
+    for key in into:
+        when(into[key], functools.partial(lambda key: pan_corner(*key).wait_recv(), key))
+    mean_stage(pe, consts, dd, down)
+    when(has_below, lambda: mean_rows(0).start())
+    when(has_above, lambda: mean_rows(1).start())
     for k in range(7, 0, -1):
         block_recv(k).wait_recv()
         when(has_below, functools.partial(lambda k: forward(k, 0).start(), k))
         when(has_above, functools.partial(lambda k: forward(k, 1).start(), k))
     own.wait()
-    for copy in const_loads:
-        copy.wait()
-    when(has_above, lambda: (pan_rows(0).wait_recv(), pan_corner(0).wait_recv()))
-    when(has_below, lambda: (pan_rows(1).wait_recv(), pan_corner(1).wait_recv()))
-    mean_stage(pe, consts, dd, down)
-    when(has_below, lambda: mean_rows(0).start())
-    when(has_above, lambda: mean_rows(1).start())
     sums[10] = pan_stage(pe, consts, d_out, ts)
     early_compute(e, consts, ts, xs, xc, ys, vl, lvp, sums)
     for k in range(8):
@@ -729,6 +773,8 @@
         total = total + g2[k]
     rt[...] = total
 
+    for key in to:
+        when(to[key], functools.partial(lambda key: pan_corner(*key).wait_send(), key))
     when(has_below, lambda: mean_rows(0).wait_send())
     when(has_above, lambda: mean_rows(1).wait_send())
     for k in range(1, 8):
@@ -739,7 +785,7 @@
     when(has_right, lambda: pan_cols(0).wait_send())
     when(has_left, lambda: pan_cols(1).wait_send())
     for side, cond in ((0, has_below), (1, has_above)):
-        when(cond, functools.partial(lambda side: (pan_rows(side).wait_send(), pan_corner(side).wait_send()), side))
+        when(cond, functools.partial(lambda side: pan_rows(side).wait_send(), side))
         for k in range(8):
             when(cond, functools.partial(lambda k, side: forward(k, side).wait_send(), k, side))
 
@@ -793,6 +839,8 @@
             pltpu.SemaphoreType.DMA((8,)),
             pltpu.SemaphoreType.DMA((16,)),
             pltpu.SemaphoreType.DMA((16,)),
+            pltpu.SemaphoreType.DMA((4,)),
+            pltpu.SemaphoreType.DMA((4,)),
         ],
         compiler_params=pltpu.CompilerParams(
             collective_id=0, has_side_effects=True, vmem_limit_bytes=56 << 20

time: 31.9 us -> 30.3 us (0.950)
  Pallas kernels: 31.1 us -> 29.5 us
    pallas_call x1, Pallas kernels: 28.8 us -> 27.2 us  [front(): pl.pallas_call(front_kernel, name='front', out_shape=[VM((8, 128), F32),...]
where the time goes in v4:
time: 30.3 us; the launch traced here: 30.2 us
  Pallas kernels  29.5 us (97%)
  between operations  0.64 us (2%)
    pallas_call x1, Pallas kernels, front(): pl.pallas_call(front_kernel, name='front', out_shape=[VM((8, 128), F32),...  27.2 us
    pallas_call x1, Pallas kernels, back(): pl.pallas_call(back_kernel, name='back', out_shape=[jax.ShapeDtypeStruct(...  2.34 us

profile of v4, /device:TPU:1, one launch (start us, length us, event | category | flops | bytes accessed | tf_op | source)
XLA Modules:
  0.0 30.2 jit_solution(4393972657203943492)
XLA Ops:
  0.6 27.2 %front.1 = (f32[8,128]{1,0:T(8,128)S(1)}, f32[384,1536]{1,0:T(8,128)S(1)}, f32[48,1536]{1,0:T(8,128)S(1)}, f32[12,8,384]{2,1,0:T(8,128)S(1)}, f32[96,384]{1,0:T(8,128)S(1)}, /*index=5*/f32[12,384]{1,0:T(8,128)S(1)}) custom-call(f32[48,1536]{1,0:T(8,128)} %pan.1, f32[288,128]{1,0:T(8,128)} %bitcast.2, f32[1,4,1024]{2,1,0:T(4,128)} %swir.1, ...), custom_call_target="tpu_custom_call" | custom-call | tf_op jit(solution)/shard_map/front/pallas_call | solution.py:794
  27.8 2.3 %back.1 = (f32[8,48,1536]{2,1,0:T(8,128)}, f32[12,8,384]{2,1,0:T(8,128)}) custom-call(f32[8,128]{1,0:T(8,128)S(1)} %get-tuple-element.10.rt, f32[384,1536]{1,0:T(8,128)S(1)} %get-tuple-element.11.up, f32[48,1536]{1,0:T(8,128)S(1)} %get-tuple-element.12.d, f32[12,8,384]{2,1,0:T(8,128)S(1)} %get-tuple-element.13.vl, f32[96,384]{1,0:T(8,128)S(1)} %get-tuple-element.14.swu, ...), custom_call_target="tpu_custom_call" | custom-call | tf_op jit(solution)/shard_map/back/pallas_call | solution.py:961

commit v5 on v4

--- a/solution.py
+++ b/solution.py
@@ -922,7 +922,7 @@
     return jnp.concatenate([x] * copies, axis=1)
 
 
-def back_kernel(rt, up, d, vl, swu, dl, joined, joined_swir, cb, gs, out, sem):
+def back_kernel(rt, up, d, vl, swu, dl, joined, joined_swir, cb, gs, out, rows_out, sem):
     gain = solve_first(rt, cb)
     for b in range(8):
         gs[b] = jnp.broadcast_to(gain[b], (8, 128))
@@ -950,11 +950,15 @@
     share3 = wide(share, 3)
     for i in range(12):
         detail = jnp.sum(v8 * vl[i], axis=0, keepdims=True) + vg * dl[i : i + 1, :]
-        joined_swir[i] = swu[8 * i : 8 * i + 8, :] + share3 * detail
+        rows_out[i] = swu[8 * i : 8 * i + 8, :] + share3 * detail
+    last = pltpu.make_async_copy(rows_out, joined_swir, sem.at[8])
+    last.start()
 
     @pl.loop(0, BANDS)
     def _(b):
         pltpu.make_async_copy(out.at[b], joined.at[b], sem.at[b]).wait()
+
+    last.wait()
 
 
 def back(rt, up, d, vl, swu, dl):
@@ -966,12 +970,13 @@
             jax.ShapeDtypeStruct((12, 8, 384), F32),
         ],
         in_specs=[pl.BlockSpec(memory_space=VM)] * 6,
-        out_specs=[pl.BlockSpec(memory_space=pl.ANY), pl.BlockSpec(memory_space=VM)],
+        out_specs=[pl.BlockSpec(memory_space=pl.ANY)] * 2,
         scratch_shapes=[
             VM((38, 8, 128), F32),
             VM((8, 8, 128), F32),
             VM((8, 48, 1536), F32),
-            pltpu.SemaphoreType.DMA((8,)),
+            VM((12, 8, 384), F32),
+            pltpu.SemaphoreType.DMA((9,)),
         ],
         compiler_params=pltpu.CompilerParams(vmem_limit_bytes=32 << 20),
     )(rt, up, d, vl, swu, dl)

time: 30.3 us -> 29.7 us (0.980)
  Pallas kernels: 29.5 us -> 28.9 us
    pallas_call x1, Pallas kernels: 2.34 us -> 1.73 us  [back(): pl.pallas_call(back_kernel, name='back', out_shape=[jax.ShapeDtypeStruct(...]
where the time goes in v5:
time: 29.7 us; the launch traced here: 29.6 us
  Pallas kernels  28.9 us (97%)
  between operations  0.64 us (2%)
    pallas_call x1, Pallas kernels, front(): pl.pallas_call(front_kernel, name='front', out_shape=[VM((8, 128), F32),...  27.2 us
    pallas_call x1, Pallas kernels, back(): pl.pallas_call(back_kernel, name='back', out_shape=[jax.ShapeDtypeStruct(...  1.73 us

profile of v5, /device:TPU:1, one launch (start us, length us, event | category | flops | bytes accessed | tf_op | source)
XLA Modules:
  0.0 29.6 jit_solution(12898280946296788659)
XLA Ops:
  0.6 27.2 %front.1 = (f32[8,128]{1,0:T(8,128)S(1)}, f32[384,1536]{1,0:T(8,128)S(1)}, f32[48,1536]{1,0:T(8,128)S(1)}, f32[12,8,384]{2,1,0:T(8,128)S(1)}, f32[96,384]{1,0:T(8,128)S(1)}, /*index=5*/f32[12,384]{1,0:T(8,128)S(1)}) custom-call(f32[48,1536]{1,0:T(8,128)} %pan.1, f32[288,128]{1,0:T(8,128)} %bitcast.2, f32[1,4,1024]{2,1,0:T(4,128)} %swir.1, ...), custom_call_target="tpu_custom_call" | custom-call | tf_op jit(solution)/shard_map/front/pallas_call | solution.py:794
  27.8 1.7 %back.1 = (f32[8,48,1536]{2,1,0:T(8,128)}, f32[12,8,384]{2,1,0:T(8,128)}) custom-call(f32[8,128]{1,0:T(8,128)S(1)} %get-tuple-element.10.rt, f32[384,1536]{1,0:T(8,128)S(1)} %get-tuple-element.11.up, f32[48,1536]{1,0:T(8,128)S(1)} %get-tuple-element.12.d, f32[12,8,384]{2,1,0:T(8,128)S(1)} %get-tuple-element.13.vl, f32[96,384]{1,0:T(8,128)S(1)} %get-tuple-element.14.swu, ...), custom_call_target="tpu_custom_call" | custom-call | tf_op jit(solution)/shard_map/back/pallas_call | solution.py:965

commit v6 on v5

--- a/solution.py
+++ b/solution.py
@@ -766,12 +766,6 @@
         sum_two(n).start()
     g2[me_two] = total
     upsample(xs, consts, zs, up_out)
-    for n in range(15):
-        sum_two_recv(n).wait_recv()
-    total = g2[0]
-    for k in range(1, 16):
-        total = total + g2[k]
-    rt[...] = total
 
     for key in to:
         when(to[key], functools.partial(lambda key: pan_corner(*key).wait_send(), key))
@@ -788,6 +782,13 @@
         when(cond, functools.partial(lambda side: pan_rows(side).wait_send(), side))
         for k in range(8):
             when(cond, functools.partial(lambda k, side: forward(k, side).wait_send(), k, side))
+
+    for n in range(15):
+        sum_two_recv(n).wait_recv()
+    total = g2[0]
+    for k in range(1, 16):
+        total = total + g2[k]
+    rt[...] = total
 
 
 def front(pan, vnir, swir):
@@ -923,6 +924,10 @@
 
 
 def back_kernel(rt, up, d, vl, swu, dl, joined, joined_swir, cb, gs, out, rows_out, sem):
+    def half_copy(b, h):
+        half = pl.ds(24 * h, 24)
+        return pltpu.make_async_copy(out.at[b, half], joined.at[b, half], sem.at[b, h])
+
     gain = solve_first(rt, cb)
     for b in range(8):
         gs[b] = jnp.broadcast_to(gain[b], (8, 128))
@@ -931,13 +936,14 @@
     def _(b):
         g = wide(gs[b], 2)
         rows = pl.multiple_of(b * 48, 48)
-        for i in range(6):
-            for t in range(6):
-                at = slice(256 * t, 256 * t + 256)
-                out[b, 8 * i : 8 * i + 8, at] = (
-                    up[pl.ds(rows + 8 * i, 8), at] + g * d[8 * i : 8 * i + 8, at]
-                )
-        pltpu.make_async_copy(out.at[b], joined.at[b], sem.at[b]).start()
+        for h in range(2):
+            for i in range(3 * h, 3 * h + 3):
+                for t in range(6):
+                    at = slice(256 * t, 256 * t + 256)
+                    out[b, 8 * i : 8 * i + 8, at] = (
+                        up[pl.ds(rows + 8 * i, 8), at] + g * d[8 * i : 8 * i + 8, at]
+                    )
+            half_copy(b, h).start()
 
     gain = [gs[b, 0:1, :] for b in range(8)]
     v, share = solve_second(rt, cb, gain)
@@ -951,12 +957,13 @@
     for i in range(12):
         detail = jnp.sum(v8 * vl[i], axis=0, keepdims=True) + vg * dl[i : i + 1, :]
         rows_out[i] = swu[8 * i : 8 * i + 8, :] + share3 * detail
-    last = pltpu.make_async_copy(rows_out, joined_swir, sem.at[8])
+    last = pltpu.make_async_copy(rows_out, joined_swir, sem.at[8, 0])
     last.start()
 
     @pl.loop(0, BANDS)
     def _(b):
-        pltpu.make_async_copy(out.at[b], joined.at[b], sem.at[b]).wait()
+        half_copy(b, 0).wait()
+        half_copy(b, 1).wait()
 
     last.wait()
 
@@ -976,7 +983,7 @@
             VM((8, 8, 128), F32),
             VM((8, 48, 1536), F32),
             VM((12, 8, 384), F32),
-            pltpu.SemaphoreType.DMA((9,)),
+            pltpu.SemaphoreType.DMA((9, 2)),
         ],
         compiler_params=pltpu.CompilerParams(vmem_limit_bytes=32 << 20),
     )(rt, up, d, vl, swu, dl)

time: 29.7 us -> 29.7 us (level)
  no operation moved by 1% of the time
where the time goes in v6:
time: 29.7 us; the launch traced here: 29.6 us
  Pallas kernels  28.9 us (97%)
  between operations  0.64 us (2%)
    pallas_call x1, Pallas kernels, front(): pl.pallas_call(front_kernel, name='front', out_shape=[VM((8, 128), F32),...  27.1 us
    pallas_call x1, Pallas kernels, back(): pl.pallas_call(back_kernel, name='back', out_shape=[jax.ShapeDtypeStruct(...  1.8 us

profile of v6, /device:TPU:1, one launch (start us, length us, event | category | flops | bytes accessed | tf_op | source)
XLA Modules:
  0.0 29.6 jit_solution(10378943897197933561)
XLA Ops:
  0.6 27.1 %front.1 = (f32[8,128]{1,0:T(8,128)S(1)}, f32[384,1536]{1,0:T(8,128)S(1)}, f32[48,1536]{1,0:T(8,128)S(1)}, f32[12,8,384]{2,1,0:T(8,128)S(1)}, f32[96,384]{1,0:T(8,128)S(1)}, /*index=5*/f32[12,384]{1,0:T(8,128)S(1)}) custom-call(f32[48,1536]{1,0:T(8,128)} %pan.1, f32[288,128]{1,0:T(8,128)} %bitcast.2, f32[1,4,1024]{2,1,0:T(4,128)} %swir.1, ...), custom_call_target="tpu_custom_call" | custom-call | tf_op jit(solution)/shard_map/front/pallas_call | solution.py:795
  27.7 1.8 %back.1 = (f32[8,48,1536]{2,1,0:T(8,128)}, f32[12,8,384]{2,1,0:T(8,128)}) custom-call(f32[8,128]{1,0:T(8,128)S(1)} %get-tuple-element.10.rt, f32[384,1536]{1,0:T(8,128)S(1)} %get-tuple-element.11.up, f32[48,1536]{1,0:T(8,128)S(1)} %get-tuple-element.12.d, f32[12,8,384]{2,1,0:T(8,128)S(1)} %get-tuple-element.13.vl, f32[96,384]{1,0:T(8,128)S(1)} %get-tuple-element.14.swu, ...), custom_call_target="tpu_custom_call" | custom-call | tf_op jit(solution)/shard_map/back/pallas_call | solution.py:972
